TPU v7x, 32 devices: a whole 2x2x4 slice. The times are simulated.
32 devices in a mesh: dp: 2 (over y), row: 4 (over x, core), col: 4 (over z).
Axes of the slice: x: 2, y: 2, z: 4, core: 2. Of those that a mesh axis runs over, the one named last changes fastest.
Arguments:
- tokens: bfloat16 [1024, 1024], P(('dp', 'row'), 'col'), may hold values from -12 to 12
- cotangent: bfloat16 [1024, 1024], P(('dp', 'row'), 'col'), may hold values from -6 to 6
- first_gain: float32 [1024], P('col'), may hold values from 0.25 to 1.75
- first_shift: float32 [1024], P('col'), may hold values from -3 to 3
- w_qkv: bfloat16 [1024, 3072], P('col', 'row'), may hold values from -0.1875 to 0.1875
- bias_qv: float32 [2048], P('row'), may hold values from -4 to 4
- w_out: bfloat16 [1024, 1024], P('row', 'col'), may hold values from -0.375 to 0.375
- bias_out: float32 [1024], P('col'), may hold values from -3 to 3
- second_gain: float32 [1024], P('col'), may hold values from 0.25 to 1.75
- second_shift: float32 [1024], P('col'), may hold values from -3 to 3
- w_up: bfloat16 [1024, 4096], P('col', 'row'), may hold values from -0.1875 to 0.1875
- bias_up: float32 [4096], P('row'), may hold values from -4 to 4
- w_down: bfloat16 [4096, 1024], P('row', 'col'), may hold values from -0.125 to 0.125
- bias_down: float32 [1024], P('col'), may hold values from -3 to 3
Outputs:
- block_out: bfloat16 [1024, 1024], P(('dp', 'row'), 'col')
- grad_tokens: float32 [1024, 1024], P(('dp', 'row'), 'col')
- grad_first_gain: float32 [1024], P('col')
- grad_first_shift: float32 [1024], P('col')
- grad_w_qkv: float32 [1024, 3072], P('col', 'row')
- grad_bias_qv: float32 [2048], P('row')
- grad_w_out: float32 [1024, 1024], P('row', 'col')
- grad_bias_out: float32 [1024], P('col')
- grad_second_gain: float32 [1024], P('col')
- grad_second_shift: float32 [1024], P('col')
- grad_w_up: float32 [1024, 4096], P('col', 'row')
- grad_bias_up: float32 [4096], P('row')
- grad_w_down: float32 [4096, 1024], P('row', 'col')
- grad_bias_down: float32 [1024], P('col')
All inputs are finite; a program needn't handle non-finite values.
Results may differ from a plain program's by a relative error of at most 0.012.
Values may be sent and summed in bfloat16 or wider, within the bound.
No kernel may reach another device: no remote copies, remote signals or barrier semaphores. Data moves between devices by JAX's collectives and lax.ppermute only.
A program may use at most 64 MiB of HBM per device.

v0:
```python
import functools

import jax
import jax.numpy as jnp
from jax import lax
from jax.experimental import pallas as pl
from jax.experimental.pallas import tpu as pltpu
from jax.sharding import PartitionSpec as P


HEADS = 16
HEAD_DIM = 64
SEQ = 512

EPS = 1e-05
GELU_C = 0.7978845608028654
GELU_A = 0.044715
BF16 = jnp.bfloat16
F32 = jnp.float32
PAD = 16
GRANT = 12 << 20


VM = pl.BlockSpec(memory_space=pltpu.VMEM)
SM = pl.BlockSpec(memory_space=pltpu.SMEM)
HB = pl.BlockSpec(memory_space=pltpu.HBM)


def call(body, outs, place, *args, flops=0, scratch=(), hbm=()):
    shapes = [jax.ShapeDtypeStruct(shape, kind) for shape, kind in outs]
    moved = sum(a.size * a.dtype.itemsize for a in args)
    moved += sum(s.size * s.dtype.itemsize for s in shapes)
    return pl.pallas_call(
        body,
        out_shape=shapes,
        in_specs=[SM] + [HB if i in hbm else VM for i in range(len(args))],
        out_specs=[VM] * len(shapes),
        scratch_shapes=list(scratch),
        compiler_params=pltpu.CompilerParams(vmem_limit_bytes=GRANT),
        cost_estimate=pl.CostEstimate(flops=flops, bytes_accessed=moved, transcendentals=0),
    )(place, *args)


def mm(left, right, left_dim, right_dim):
    return lax.dot_general(
        left, right, (((left_dim,), (right_dim,)), ((), ())), preferred_element_type=F32
    )


def part(index, extent):
    return pl.ds(pl.multiple_of(index * extent, extent), extent)


def source(place, step, cols):
    return lax.rem(place[0] + cols - step, cols)


def target(place, step, cols):
    return lax.rem(place[0] + step, cols)


def split_rows(values):
    high = values.astype(BF16)
    return (high, (values - high.astype(F32)).astype(BF16))


def block_order(rows):
    order = [0]
    bit = rows // 2
    while bit:
        order = order + [o ^ bit for o in order]
        bit //= 2
    return order


def positions(place, order, extent, axis):
    shape = (extent, 1) if axis == 0 else (1, extent)
    pieces = [
        lax.broadcasted_iota(jnp.int32, shape, axis) + jnp.bitwise_xor(place[1], o) * extent
        for o in order
    ]
    return pieces if axis == 0 else jnp.concatenate(pieces, axis)


def shift(block, axis, step):
    size = lax.axis_size(axis)
    return lax.ppermute(block, axis, [(i, (i + step) % size) for i in range(size)])


def swap(block, axis, bit):
    size = lax.axis_size(axis)
    return lax.ppermute(block, axis, [(i, i ^ bit) for i in range(size)])


def exchange(blocks):
    return [blocks[0]] + [shift(blocks[s], "col", s) for s in range(1, len(blocks))]


def gather_row(block):
    pieces = [block]
    bit = lax.axis_size("row") // 2
    while bit:
        for i in range(len(pieces)):
            pieces = pieces + [swap(pieces[i], "row", bit)]
        bit //= 2
    return pieces


def sum_small(small, axis):
    bit = 1
    while bit < lax.axis_size(axis):
        small = small + swap(small, axis, bit)
        bit *= 2
    return small


def swap_dp(message):
    size = lax.axis_size("dp")
    bit = 1
    while bit < size // 2:
        message = (message.astype(F32) + swap(message, "dp", bit).astype(F32)).astype(BF16)
        bit *= 2
    return (message, swap(message, "dp", bit))


def head_kernel(tokens, vectors, out):
    rows = tokens.shape[0]
    out[:rows] = tokens[...]
    high, low = split_rows(vectors[...])
    out[rows:] = jnp.concatenate([high.astype(F32), low.astype(F32)], 0).astype(BF16)


def qkv_pieces_kernel(place, w_qkv_hbm, w_out_hbm, *refs):
    outs, (w_qkv, w_out, sems) = refs[:-3], refs[-3:]
    copies = [
        pltpu.make_async_copy(w_qkv_hbm, w_qkv, sems.at[0]),
        pltpu.make_async_copy(w_out_hbm, w_out, sems.at[1]),
    ]
    for copy in copies:
        copy.start()
    for copy in copies:
        copy.wait()
    cols = len(outs)
    width = w_qkv.shape[1] // cols
    height = w_out.shape[0] // cols
    for step, out in enumerate(outs):
        for k in range(cols):

            @pl.when(target(place, step, cols) == k)
            def _(out=out, k=k):
                out[:, :width] = w_qkv[:, k * width : (k + 1) * width]
                out[:, width:] = w_out[k * height : (k + 1) * height].astype(F32).T.astype(BF16)


def ff_pieces_kernel(place, cotangent, w_up, w_down, *refs):
    outs, sems = refs[:-1], refs[-1]
    cols = len(outs)
    width = w_up.shape[1] // cols
    high = w_up.shape[0]
    copies = []
    for step, out in enumerate(outs):
        index = target(place, step, cols)
        pairs = [
            (w_up.at[:, part(index, width)], out.at[:high]),
            (w_down.at[part(index, width), :], out.at[high : high + width]),
            (cotangent, out.at[high + width :]),
        ]
        for i, (there, here) in enumerate(pairs):
            copies.append(pltpu.make_async_copy(there, here, sems.at[3 * step + i]))
    for copy in copies:
        copy.start()
    for copy in copies:
        copy.wait()


def first_norm_kernel(place, *refs):
    cols = (len(refs) - 5) // 1
    pieces, (first_in, normed_out, rstd_out, x_out, vec_out) = refs[:cols], refs[cols:]
    rows = first_in.shape[0]
    feats = pieces[0].shape[1]
    for step, piece in enumerate(pieces):
        at = part(source(place, step, cols), feats)
        x_out[:, at] = piece[:rows]
        tail = piece[rows:].astype(F32)
        vec_out[:, at] = tail[:8] + tail[8:]
    x = x_out[...].astype(F32)
    width = x.shape[1]
    centre = jnp.sum(x, 1, keepdims=True) / width
    spread = jnp.sum(x * x, 1, keepdims=True) / width - centre * centre
    rstd = lax.rsqrt(spread + EPS)
    normed = (x - centre) * rstd
    normed_out[...] = normed
    rstd_out[...] = rstd
    first_in[...] = (normed * vec_out[0:1] + vec_out[1:2]).astype(BF16)


def attention_kernel(order, heads, cols, place, slopes, bias, *refs):
    rows = len(order)
    first, weights = refs[:rows], refs[rows : rows + cols]
    q_out, k_out, v_out, log_out, ctx_out, wq_out, wo_out, keep, send = refs[rows + cols :]
    feats = weights[0].shape[0]
    width = wq_out.shape[1]
    for step, piece in enumerate(weights):
        at = part(source(place, step, cols), feats)
        wq_out[at, :] = piece[:, :width]
        wo_out[at, :] = piece[:, width:]
    extent = first[0].shape[0]
    own_bias = bias[:, part(place[0], 2 * heads * HEAD_DIM)]
    for p in range(rows):
        joined = mm(first[p][...], wq_out[...], 1, 0)
        at = slice(p * extent, (p + 1) * extent)
        for h in range(heads):
            here = slice(h * HEAD_DIM, (h + 1) * HEAD_DIM)
            base = 3 * h * HEAD_DIM
            b = 2 * h * HEAD_DIM
            q = joined[:, base : base + HEAD_DIM] + own_bias[:, b : b + HEAD_DIM]
            v = joined[:, base + 2 * HEAD_DIM : base + 3 * HEAD_DIM]
            v = v + own_bias[:, b + HEAD_DIM : b + 2 * HEAD_DIM]
            q_out[at, here] = q.astype(BF16)
            k_out[at, here] = joined[:, base + HEAD_DIM : base + 2 * HEAD_DIM].astype(BF16)
            v_out[at, here] = v.astype(BF16)
    for p in range(rows):
        at = slice(p * extent, (p + 1) * extent)
        for h in range(heads):
            here = slice(h * HEAD_DIM, (h + 1) * HEAD_DIM)
            scores = block_scores(place, order, extent, p, q_out[at, here], k_out[:, here], slopes[h])
            expo = jnp.exp(scores)
            total = jnp.sum(expo, 1, keepdims=True)
            log_out[at, h : h + 1] = jnp.log(total)
            numerator = mm(expo.astype(BF16), v_out[:, here], 1, 0)
            ctx_out[at, here] = (numerator / total).astype(BF16)
    half = keep.shape[0]
    keep[...] = mm(ctx_out[:half], wo_out[...], 1, 1)
    send[...] = mm(ctx_out[half:], wo_out[...], 1, 1).astype(BF16)


def block_scores(place, order, extent, p, query, keys, slope):
    query_pos = positions(place, order[p : p + 1], extent, 0)[0]
    key_pos = positions(place, order, extent, 1)
    offsets = query_pos - key_pos
    same = lax.div(query_pos, jnp.int32(SEQ)) == lax.div(key_pos, jnp.int32(SEQ))
    scores = mm(query, keys, 1, 1) * 0.125 - slope * offsets.astype(F32)
    return jnp.where((offsets >= 0) & same, scores, -30000.0)


def probs_kernel(order, heads, place, slopes, q, k, logs, out):
    rows = len(order)
    extent = q.shape[0] // rows
    for h in range(heads):
        here = slice(h * HEAD_DIM, (h + 1) * HEAD_DIM)
        for p in range(rows):
            at = slice(p * extent, (p + 1) * extent)
            scores = block_scores(place, order, extent, p, q[at, here], k[:, here], slopes[h])
            out[h, at, :] = jnp.exp(scores - logs[at, h : h + 1])


def fold_kernel(place, keep, recv, keep_out, send_out):
    half = keep_out.shape[0]
    keep_out[...] = keep[:half] + recv[:half].astype(F32)
    send_out[...] = (keep[half:] + recv[half:].astype(F32)).astype(BF16)


def to_tokens_kernel(place, keep, recv, own, *sends):
    cols = len(sends) + 1
    count = own.shape[0]
    for step, out in enumerate((own, *sends)):
        at = part(target(place, step, cols), count)
        out[...] = (keep[at, :] + recv[at, :].astype(F32)).astype(out.dtype)


def total_of(own, received):
    total = own[...]
    for piece in received:
        total = total + piece[...].astype(F32)
    return total


def second_norm_kernel(place, own, *refs):
    received, (x, vec, resid_out, normed_out, rstd_out, second_in) = refs[:-6], refs[-6:]
    count = own.shape[0]
    x_own = x[part(place[0], count), :].astype(F32)
    resid = x_own + total_of(own, received) + vec[2:3]
    width = resid.shape[1]
    centre = jnp.sum(resid, 1, keepdims=True) / width
    spread = jnp.sum(resid * resid, 1, keepdims=True) / width - centre * centre
    rstd = lax.rsqrt(spread + EPS)
    normed = (resid - centre) * rstd
    resid_out[...] = resid
    normed_out[...] = normed
    rstd_out[...] = rstd
    second_in[...] = (normed * vec[3:4] + vec[4:5]).astype(BF16)


def join_rows_kernel(place, *refs):
    pieces, out = refs[:-1], refs[-1]
    count = pieces[0].shape[0]
    for step, piece in enumerate(pieces):
        out[part(source(place, step, len(pieces)), count), :] = piece[...]


def ff_join_kernel(place, *refs):
    pieces, (up_out, down_out, cot_out) = refs[:-3], refs[-3:]
    cols = len(pieces)
    feats = pieces[0].shape[1] if cot_out.shape[1] == cols * pieces[0].shape[1] else 0
    high = up_out.shape[0] // cols
    width = down_out.shape[0]
    for step, piece in enumerate(pieces):
        at = part(source(place, step, cols), feats)
        up_out[at, :] = piece[:high]
        down_out[:, at] = piece[high : high + width]
        cot_out[:, at] = piece[high + width :]


def cot_kernel(place, down, *refs):
    pieces, out = refs[:-1], refs[-1]
    extent = pieces[0].shape[0]
    for p, piece in enumerate(pieces):
        out[p * extent : (p + 1) * extent] = mm(piece[...], down[...], 1, 1)


def hidden_kernel(place, up, bias, cot_down, *refs):
    pieces, (act_out, grad_out, bias_out, keep, send) = refs[:-5], refs[-5:]
    extent = pieces[0].shape[0]
    width = up.shape[1]
    own_bias = bias[:, part(place[0], width)]
    bias_total = jnp.zeros((1, width), F32)
    for p, piece in enumerate(pieces):
        at = slice(p * extent, (p + 1) * extent)
        hidden = mm(piece[...], up[...], 1, 0) + own_bias
        inner = GELU_C * (hidden + GELU_A * hidden * hidden * hidden)
        tanh_val = jnp.tanh(inner)
        act_out[at] = (0.5 * hidden * (1.0 + tanh_val)).astype(BF16)
        slope = 0.5 * (1.0 + tanh_val) + 0.5 * hidden * (1.0 - tanh_val * tanh_val) * GELU_C * (
            1.0 + 3.0 * GELU_A * hidden * hidden
        )
        grad_pre = cot_down[at] * slope
        bias_total = bias_total + jnp.sum(grad_pre, 0, keepdims=True)
        grad_out[at] = grad_pre.astype(BF16)
    bias_out[...] = bias_total
    half = keep.shape[0]
    keep[...] = mm(grad_out[:half], up[...], 1, 1)
    send[...] = mm(grad_out[half:], up[...], 1, 1).astype(BF16)


def out_part_kernel(place, act, down, keep, send):
    half = keep.shape[0]
    keep[...] = mm(act[:half], down[...], 1, 0)
    send[...] = mm(act[half:], down[...], 1, 0).astype(BF16)


def out_features_kernel(place, keep, recv, resid, own, *refs):
    sends, total = refs[:-1], refs[-1]
    cols = len(sends) + 1
    feats = own.shape[1]
    total[...] = keep[...] + recv[...].astype(F32)
    mine = part(place[0], resid.shape[0])
    total[mine, :] = total[mine, :] + resid[...]
    for step, out in enumerate((own, *sends)):
        out[...] = total[:, part(target(place, step, cols), feats)].astype(out.dtype)


def block_out_kernel(place, bias, own, *refs):
    received, out = refs[:-1], refs[-1]
    out[...] = (total_of(own, received) + bias[...]).astype(BF16)


def ff_grad_kernel(rows, cols, place, act, grad, bias, *refs):
    second, cots, out = refs[:rows], refs[rows : 2 * rows], refs[-1]
    extent = second[0].shape[0]
    feats = second[0].shape[1] // cols
    width = grad.shape[1]
    stride = feats + width
    for j in range(cols):
        here = slice(j * feats, (j + 1) * feats)
        up = jnp.zeros((feats, width), F32)
        down = jnp.zeros((width, feats), F32)
        for p in range(rows):
            at = slice(p * extent, (p + 1) * extent)
            up = up + mm(second[p][:, here], grad[at], 0, 0)
            down = down + mm(act[at], cots[p][:, here], 0, 0)
        out[j * stride : j * stride + feats] = up.astype(BF16)
        out[j * stride + feats : (j + 1) * stride] = down.astype(BF16)
    out[cols * stride :] = pair_rows(bias[...])


def pair_rows(vector):
    high, low = split_rows(vector)
    empty = jnp.zeros((PAD - 2, vector.shape[1]), F32)
    return jnp.concatenate([high.astype(F32), low.astype(F32), empty], 0).astype(BF16)


def dp_sum_kernel(place, mine, other, own, *sends):
    cols = len(sends) + 1
    stride = own.shape[0] - PAD
    tail = cols * stride
    ends = mine[tail:].astype(F32) + other[tail:].astype(F32)
    both = ends[0:1] + ends[1:2]
    for step, out in enumerate((own, *sends)):
        at = part(target(place, step, cols), stride)
        out[:stride] = (mine[at, :].astype(F32) + other[at, :].astype(F32)).astype(out.dtype)
        out[stride:] = pair_rows(both).astype(out.dtype)


def ff_final_kernel(place, *refs):
    pieces, (up_out, down_out, bias_out) = refs[:-3], refs[-3:]
    cols = len(pieces)
    feats = down_out.shape[1]
    width = up_out.shape[1] // cols
    for step, piece in enumerate(pieces):
        at = part(source(place, step, cols), width)
        up_out[:, at] = piece[:feats].astype(F32)
        down_out[at, :] = piece[feats : feats + width].astype(F32)
        tail = piece[feats + width :].astype(F32)
        bias_out[:, at] = tail[0:1] + tail[1:2]


def second_back_kernel(place, own, *refs):
    received = refs[:-7]
    normed, rstd, vec, cot, resid_out, resid_b, sums = refs[-7:]
    count = own.shape[0]
    grad = total_of(own, received)
    n = normed[...]
    width = grad.shape[1]
    scaled = grad * vec[3:4]
    mean_one = jnp.sum(scaled, 1, keepdims=True) / width
    mean_two = jnp.sum(scaled * n, 1, keepdims=True) / width
    cot_own = cot[part(place[0], count), :].astype(F32)
    resid = cot_own + rstd[...] * (scaled - mean_one - n * mean_two)
    resid_out[...] = resid
    resid_b[...] = resid.astype(BF16)
    sums[0:1] = jnp.sum(grad * n, 0, keepdims=True)
    sums[1:2] = jnp.sum(grad, 0, keepdims=True)
    sums[2:3] = jnp.sum(resid, 0, keepdims=True)
    sums[3:4] = jnp.sum(cot_own, 0, keepdims=True)
    sums[4:8] = jnp.zeros((4, width), F32)


def attention_back_kernel(rows, heads, place, wq, wo, q, k, v, ctx, probs, *refs):
    resid = refs[:rows]
    joined_out, bias_out, keep, send, gctx = refs[rows:]
    extent = resid[0].shape[0]
    for p in range(rows):
        at = slice(p * extent, (p + 1) * extent)
        gctx[at] = mm(resid[p][...], wo[...], 1, 0).astype(BF16)
    for h in range(heads):
        here = slice(h * HEAD_DIM, (h + 1) * HEAD_DIM)
        base = 3 * h * HEAD_DIM
        size = q.shape[0]
        grad_k = jnp.zeros((size, HEAD_DIM), F32)
        grad_v = jnp.zeros((size, HEAD_DIM), F32)
        bias_q = jnp.zeros((1, HEAD_DIM), F32)
        for p in range(rows):
            at = slice(p * extent, (p + 1) * extent)
            grad = gctx[at, here]
            delta = jnp.sum(grad.astype(F32) * ctx[at, here].astype(F32), 1, keepdims=True)
            prob = probs[h, at, :]
            dscore = (prob * (mm(grad, v[:, here], 1, 1) - delta)).astype(BF16)
            grad_q = mm(dscore, k[:, here], 1, 0) * 0.125
            bias_q = bias_q + jnp.sum(grad_q, 0, keepdims=True)
            joined_out[at, base : base + HEAD_DIM] = grad_q.astype(BF16)
            grad_k = grad_k + mm(dscore, q[at, here], 0, 0)
            grad_v = grad_v + mm(prob.astype(BF16), grad, 0, 0)
        joined_out[:, base + HEAD_DIM : base + 2 * HEAD_DIM] = (grad_k * 0.125).astype(BF16)
        joined_out[:, base + 2 * HEAD_DIM : base + 3 * HEAD_DIM] = grad_v.astype(BF16)
        b = 2 * h * HEAD_DIM
        bias_out[:, b : b + HEAD_DIM] = bias_q
        bias_out[:, b + HEAD_DIM : b + 2 * HEAD_DIM] = jnp.sum(grad_v, 0, keepdims=True)
    half = keep.shape[0]
    keep[...] = mm(joined_out[:half], wq[...], 1, 1)
    send[...] = mm(joined_out[half:], wq[...], 1, 1).astype(BF16)


def qkv_grad_kernel(rows, place, joined, ctx, bias, *refs):
    first, resid, out = refs[:rows], refs[rows : 2 * rows], refs[-1]
    extent = first[0].shape[0]
    width = joined.shape[1]
    high = first[0].shape[1]
    grad = jnp.zeros((high, width), F32)
    grad_out = jnp.zeros((high, ctx.shape[1]), F32)
    for p in range(rows):
        at = slice(p * extent, (p + 1) * extent)
        grad = grad + mm(first[p][...], joined[at], 0, 0)
        grad_out = grad_out + mm(resid[p][...], ctx[at], 0, 0)
    out[:high, :width] = grad.astype(BF16)
    out[:high, width:] = grad_out.astype(BF16)
    rest = out.shape[1] - bias.shape[1]
    row = jnp.concatenate([bias[...], jnp.zeros((1, rest), F32)], 1)
    out[high:] = pair_rows(row)


def qkv_final_kernel(place, *refs):
    pieces, (qkv_out, out_out, bias_out) = refs[:-3], refs[-3:]
    cols = len(pieces)
    feats = qkv_out.shape[0]
    width = qkv_out.shape[1] // cols
    high = out_out.shape[0] // cols
    bias = bias_out.shape[1] // cols
    for step, piece in enumerate(pieces):
        index = source(place, step, cols)
        for k in range(cols):

            @pl.when(index == k)
            def _(piece=piece, k=k):
                qkv_out[:, k * width : (k + 1) * width] = piece[:feats, :width].astype(F32)

        out_out[part(index, high), :] = piece[:feats, width:].astype(F32).T
        tail = piece[feats:, :bias].astype(F32)
        bias_out[:, part(index, bias)] = tail[0:1] + tail[1:2]


def first_back_kernel(place, keep, recv, normed, rstd, vec, resid, sums, own, *refs):
    sends, total = refs[:-1], refs[-1]
    cols = len(sends) + 1
    feats = own.shape[1]
    extent, width = keep.shape
    grad = keep[...] + recv[...].astype(F32)
    n = normed[...]
    scaled = grad * vec[0:1]
    one = jnp.sum(scaled, 1, keepdims=True) / width
    two = jnp.sum(scaled * n, 1, keepdims=True) / width
    total[:extent] = rstd[...] * scaled
    mine = part(place[0], resid.shape[0])
    total[mine, :] = total[mine, :] + resid[...]
    gain_sum = jnp.sum(grad * n, 0, keepdims=True)
    shift_sum = jnp.sum(grad, 0, keepdims=True)
    lane = lax.broadcasted_iota(jnp.int32, (extent, 128), 1)
    stats = jnp.where(lane == 0, one, jnp.where(lane == 1, two, 0.0)).T[:2]
    stats = jnp.concatenate([stats, jnp.zeros((2, feats - extent), F32)], 1)
    tail = total.at[extent : extent + 8]
    tail[0:4] = sums[0:4]
    tail[4:5] = gain_sum
    tail[5:6] = shift_sum
    for step, out in enumerate((own, *sends)):
        at = part(target(place, step, cols), feats)
        out[:extent] = total[:extent, at].astype(out.dtype)
        ends = jnp.concatenate([tail[0:6, at], stats], 0)
        high, low = split_rows(ends)
        out[extent:] = jnp.concatenate([high.astype(F32), low.astype(F32)], 0).astype(out.dtype)


def tokens_final_kernel(place, normed, rstd, own, *refs):
    received, (out, sums) = refs[:-2], refs[-2:]
    extent, feats = out.shape
    total = total_of(own, received)
    ends = total[extent : extent + 8] + total[extent + 8 : extent + 16]
    sums[...] = ends
    lanes = jnp.concatenate([ends[6:8, :extent], jnp.zeros((6, extent), F32)], 0)
    square = jnp.concatenate([lanes, jnp.zeros((120, extent), F32)], 0).T
    n = normed[:, part(place[0], feats)]
    out[...] = total[:extent] - rstd[...] * (square[:, 0:1] + n * square[:, 1:2])


def scatter_row(keep, send, place):
    bit = 1
    while bit < lax.axis_size("row") // 2:
        recv = swap(send, "row", bit)
        half = (keep.shape[0] // 2, keep.shape[1])
        keep, send = call(fold_kernel, [(half, F32), (half, BF16)], place, keep, recv)
        bit *= 2
    return (keep, swap(send, "row", bit))


def local(
    tokens,
    cotangent,
    first_gain,
    first_shift,
    w_qkv,
    bias_qv,
    w_out,
    bias_out,
    second_gain,
    second_shift,
    w_up,
    bias_up,
    w_down,
    bias_down,
):
    cols = lax.axis_size("col")
    rows = lax.axis_size("row")
    own_col = lax.axis_index("col")
    own_row = lax.axis_index("row")
    place = jnp.stack([own_col, own_row]).astype(jnp.int32)
    extent, feats = tokens.shape
    width = feats * cols
    group = extent * rows
    half = group // 2
    count = extent // cols
    head_count = bias_qv.shape[0] // (2 * HEAD_DIM)
    heads = head_count // cols
    qkv_cols = w_qkv.shape[1] // cols
    ff_cols = w_up.shape[1] // cols
    out_rows = w_out.shape[0] // cols
    order = block_order(rows)
    head_ids = own_row * head_count + own_col * heads + jnp.arange(heads, dtype=jnp.int32)
    slopes = jnp.exp2(-8.0 * (head_ids.astype(F32) + 1.0) / HEADS)

    vectors = [first_gain, first_shift, bias_out, second_gain, second_shift]
    vectors = jnp.stack(vectors + [jnp.zeros_like(first_gain)] * (8 - len(vectors)))
    head_block = pl.pallas_call(
        head_kernel,
        out_shape=jax.ShapeDtypeStruct((extent + PAD, feats), BF16),
        in_specs=[VM, VM],
        out_specs=VM,
        compiler_params=pltpu.CompilerParams(vmem_limit_bytes=GRANT),
        name="head",
    )(tokens, vectors)
    heads_in = exchange([head_block] * cols)
    qkv_blocks = call(
        qkv_pieces_kernel,
        [((feats, qkv_cols + out_rows), BF16)] * cols,
        place,
        w_qkv,
        w_out,
        hbm=(0, 1),
        scratch=[
            pltpu.VMEM(w_qkv.shape, BF16),
            pltpu.VMEM(w_out.shape, BF16),
            pltpu.SemaphoreType.DMA((2,)),
        ],
    )
    qkv_in = exchange(qkv_blocks)
    first_in, normed_one, rstd_one, x_rows, vec = call(
        first_norm_kernel,
        [
            ((extent, width), BF16),
            ((extent, width), F32),
            ((extent, 1), F32),
            ((extent, width), BF16),
            ((8, width), F32),
        ],
        place,
        *heads_in,
    )
    first_all = gather_row(first_in)

    cot_late, up_late, down_late = lax.optimization_barrier(
        (cotangent, w_up, w_down, first_in)
    )[:3]
    ff_blocks = call(
        ff_pieces_kernel,
        [((feats + ff_cols + extent, feats), BF16)] * cols,
        place,
        cot_late,
        up_late,
        down_late,
        hbm=(0, 1, 2),
        scratch=[pltpu.SemaphoreType.DMA((3 * cols,))],
    )
    ff_in = exchange(ff_blocks)

    wide = (group, heads * HEAD_DIM)
    partial_outs = [((half, width), F32), ((half, width), BF16)]
    body = functools.partial(attention_kernel, order, heads, cols)

    def attention_body(place_ref, slopes_ref, *refs):
        body(place_ref, slopes_ref, *refs)

    q, k, v, logs, context, wq, wo, keep, send = call_slopes(
        attention_body,
        [
            (wide, BF16),
            (wide, BF16),
            (wide, BF16),
            ((group, heads), F32),
            (wide, BF16),
            ((width, qkv_cols), BF16),
            ((width, out_rows), BF16),
        ]
        + partial_outs,
        place,
        slopes,
        bias_qv.reshape(1, -1),
        *first_all,
        *qkv_in,
    )
    keep, recv = scatter_row(keep, send, place)
    own, *sends = call(
        to_tokens_kernel,
        [((count, width), F32)] + [((count, width), BF16)] * (cols - 1),
        place,
        keep,
        recv,
    )
    received = exchange([own, *sends])[1:]
    resid, normed_two, rstd_two, second_in = call(
        second_norm_kernel,
        [
            ((count, width), F32),
            ((count, width), F32),
            ((count, 1), F32),
            ((count, width), BF16),
        ],
        place,
        own,
        *received,
        x_rows,
        vec,
    )
    (second_rows,) = call(
        join_rows_kernel, [((extent, width), BF16)], place, *exchange([second_in] * cols)
    )
    second_all = gather_row(second_rows)

    w_up_s, w_down_s, cot_rows = call(
        ff_join_kernel,
        [((width, ff_cols), BF16), ((ff_cols, width), BF16), ((extent, width), BF16)],
        place,
        *ff_in,
    )
    cot_all = gather_row(cot_rows)
    (cot_down,) = call(
        cot_kernel,
        [((group, ff_cols), F32)],
        place,
        w_down_s,
        *cot_all,
        flops=2 * group * width * ff_cols,
    )
    (probs,) = call_slopes(
        functools.partial(probs_kernel, order, heads),
        [((heads, group, group), F32)],
        place,
        slopes,
        q,
        k,
        logs,
    )

    act, grad_pre, up_bias_part, keep, send = call(
        hidden_kernel,
        [((group, ff_cols), BF16), ((group, ff_cols), BF16), ((1, ff_cols), F32)] + partial_outs,
        place,
        w_up_s,
        bias_up.reshape(1, -1),
        cot_down,
        *second_all,
        flops=4 * group * width * ff_cols,
    )
    keep, recv = scatter_row(keep, send, place)
    own, *sends = call(
        to_tokens_kernel,
        [((count, width), F32)] + [((count, width), BF16)] * (cols - 1),
        place,
        keep,
        recv,
    )
    received = exchange([own, *sends])[1:]
    grad_resid, resid_b, sums = call(
        second_back_kernel,
        [((count, width), F32), ((count, width), BF16), ((8, width), F32)],
        place,
        own,
        *received,
        normed_two,
        rstd_two,
        vec,
        cot_rows,
    )
    (resid_rows,) = call(
        join_rows_kernel, [((extent, width), BF16)], place, *exchange([resid_b] * cols)
    )
    resid_all = gather_row(resid_rows)

    keep, send = call(
        out_part_kernel, partial_outs, place, act, w_down_s, flops=2 * group * width * ff_cols
    )
    keep, recv = scatter_row(keep, send, place)
    own, *sends = call(
        out_features_kernel,
        [((extent, feats), F32)] + [((extent, feats), BF16)] * (cols - 1),
        place,
        keep,
        recv,
        resid,
        scratch=[pltpu.VMEM((extent, width), F32)],
    )
    (block_out,) = call(
        block_out_kernel,
        [((extent, feats), BF16)],
        place,
        bias_down.reshape(1, -1),
        own,
        *exchange([own, *sends])[1:],
    )

    (ff_message,) = call(
        functools.partial(ff_grad_kernel, rows, cols),
        [((cols * (feats + ff_cols) + PAD, ff_cols), BF16)],
        place,
        act,
        grad_pre,
        up_bias_part,
        *second_all,
        *cot_all,
        flops=4 * group * width * ff_cols,
    )
    ff_shape = (feats + ff_cols + PAD, ff_cols)
    ff_sums = call(
        dp_sum_kernel,
        [(ff_shape, F32)] + [(ff_shape, BF16)] * (cols - 1),
        place,
        *swap_dp(ff_message),
    )
    grad_w_up, grad_w_down, grad_bias_up = call(
        ff_final_kernel,
        [(w_up.shape, F32), (w_down.shape, F32), ((1, bias_up.shape[0]), F32)],
        place,
        *exchange(ff_sums),
    )

    joined, qv_bias_part, keep, send = call(
        functools.partial(attention_back_kernel, rows, heads),
        [((group, qkv_cols), BF16), ((1, 2 * heads * HEAD_DIM), F32)] + partial_outs,
        place,
        wq,
        wo,
        q,
        k,
        v,
        context,
        probs,
        *resid_all,
        scratch=[pltpu.VMEM(wide, BF16)],
    )
    (qkv_message,) = call(
        functools.partial(qkv_grad_kernel, rows),
        [((width + PAD, qkv_cols + out_rows), BF16)],
        place,
        joined,
        context,
        qv_bias_part,
        *first_all,
        *resid_all,
        flops=2 * group * width * (qkv_cols + out_rows),
    )
    qkv_shape = (feats + PAD, qkv_cols + out_rows)
    qkv_sums = call(
        dp_sum_kernel,
        [(qkv_shape, F32)] + [(qkv_shape, BF16)] * (cols - 1),
        place,
        *swap_dp(qkv_message),
    )
    grad_w_qkv, grad_w_out, grad_bias_qv = call(
        qkv_final_kernel,
        [(w_qkv.shape, F32), (w_out.shape, F32), ((1, bias_qv.shape[0]), F32)],
        place,
        *exchange(qkv_sums),
    )

    keep, recv = scatter_row(keep, send, place)
    last_shape = (extent + PAD, feats)
    last = call(
        first_back_kernel,
        [(last_shape, F32)] + [(last_shape, BF16)] * (cols - 1),
        place,
        keep,
        recv,
        normed_one,
        rstd_one,
        vec,
        grad_resid,
        sums,
        scratch=[pltpu.VMEM((extent + 8, width), F32)],
    )
    grad_tokens, col_sums = call(
        tokens_final_kernel,
        [((extent, feats), F32), ((8, feats), F32)],
        place,
        normed_one,
        rstd_one,
        *exchange(last),
    )
    col_sums = sum_small(sum_small(col_sums, "row"), "dp")

    return (
        block_out,
        grad_tokens,
        col_sums[4],
        col_sums[5],
        grad_w_qkv,
        grad_bias_qv.reshape(-1),
        grad_w_out,
        col_sums[2],
        col_sums[0],
        col_sums[1],
        grad_w_up,
        grad_bias_up.reshape(-1),
        grad_w_down,
        col_sums[3],
    )


def call_slopes(body, outs, place, slopes, *args):
    shapes = [jax.ShapeDtypeStruct(shape, kind) for shape, kind in outs]
    moved = sum(a.size * a.dtype.itemsize for a in args)
    moved += sum(s.size * s.dtype.itemsize for s in shapes)
    return pl.pallas_call(
        body,
        out_shape=shapes,
        in_specs=[SM, SM] + [VM] * len(args),
        out_specs=[VM] * len(shapes),
        compiler_params=pltpu.CompilerParams(vmem_limit_bytes=GRANT),
        cost_estimate=pl.CostEstimate(flops=1 << 31, bytes_accessed=moved, transcendentals=1 << 19),
    )(place, slopes, *args)


def solution(mesh):
    tokens_spec = P(("dp", "row"), "col")
    vector = P("col")
    placed = (
        tokens_spec,
        tokens_spec,
        vector,
        vector,
        P("col", "row"),
        P("row"),
        P("row", "col"),
        vector,
        vector,
        vector,
        P("col", "row"),
        P("row"),
        P("row", "col"),
        vector,
    )


    return jax.shard_map(
        local,
        mesh=mesh,
        in_specs=placed,
        out_specs=(
            tokens_spec,
            tokens_spec,
            vector,
            vector,
            P("col", "row"),
            P("row"),
            P("row", "col"),
            vector,
            vector,
            vector,
            P("col", "row"),
            P("row"),
            P("row", "col"),
            vector,
        ),
        check_vma=False,
    )
```

profile of v0, /device:TPU:0, one launch (start us, length us, event | category | flops | bytes accessed | tf_op | source)
XLA Modules:
  0.0 220.3 jit_solution(16268060524136177273)
XLA Ops:
  2.3 3.1 %collective-permute-start = (bf16[144,256]{1,0:T(8,128)(2,1)S(1)}, bf16[144,256]{1,0:T(8,128)(2,1)S(1)}, u32[]{:S(2)}, u32[]{:S(2)}) collective-permute-start(bf16[144,256]{1,0:T(8,128)(2,1)S(1)} %head.1.refs_0_), channel_id=1, source_target_pairs={{0,1},{1,2},{2,3},{3,0},{4,5},{5,6},{6,7},{7,4},{8,9},{9,10},{10,1... | collective-permute-start | bytes 221192 | tf_op jit(solution)/shard_map/ppermute | solution.py:87
  5.4 2.6 %collective-permute-start.1 = (bf16[144,256]{1,0:T(8,128)(2,1)S(1)}, bf16[144,256]{1,0:T(8,128)(2,1)S(1)}, u32[]{:S(2)}, u32[]{:S(2)}) collective-permute-start(bf16[144,256]{1,0:T(8,128)(2,1)S(1)} %head.1.refs_0_), channel_id=1, source_target_pairs={{0,2},{1,3},{2,0},{3,1},{4,6},{5,7},{6,4},{7,5},{8,10},{9,11},{10,... | collective-permute-start | bytes 221192 | tf_op jit(solution)/shard_map/ppermute | solution.py:87
  8.0 1.3 collective-permute-start.2
  10.1 2.9 %collective-permute-done.1.refs_2_ = bf16[144,256]{1,0:T(8,128)(2,1)S(1)} collective-permute-done((bf16[144,256]{1,0:T(8,128)(2,1)S(1)}, bf16[144,256]{1,0:T(8,128)(2,1)S(1)}, u32[]{:S(2)}, u32[]{:S(2)}) %collective-permute-start.1) | collective-permute-done | bytes 73760 | tf_op jit(solution)/shard_map/ppermute | solution.py:87
  14.0 1.6 collective-permute-start.9
  15.5 6.4 %collective-permute-done.9.refs_2_.refs_1_ = bf16[128,1024]{1,0:T(8,128)(2,1)S(1)} collective-permute-done((bf16[128,1024]{1,0:T(8,128)(2,1)S(1)}, bf16[128,1024]{1,0:T(8,128)(2,1)S(1)}, u32[]{:S(2)}, u32[]{:S(2)}) %collective-permute-start.9) | collective-permute-done | bytes 262176 | tf_op jit(solution)/shard_map/ppermute | solution.py:92
  23.8 1.8 shard_map.249
  25.7 2.2 collective-permute-start.12
  27.9 1.2 collective-permute-start.13
  29.0 1.3 collective-permute-start.14
  30.4 3.7 %collective-permute-done.12.refs_6_ = bf16[256,256]{1,0:T(8,128)(2,1)S(1)} collective-permute-done((bf16[256,256]{1,0:T(8,128)(2,1)S(1)}, bf16[256,256]{1,0:T(8,128)(2,1)S(1)}, u32[]{:S(2)}, u32[]{:S(2)}) %collective-permute-start.12) | collective-permute-done | bytes 131104 | tf_op jit(solution)/shard_map/ppermute | solution.py:87
  34.0 5.1 %collective-permute-done.13.refs_7_ = bf16[256,256]{1,0:T(8,128)(2,1)S(1)} collective-permute-done((bf16[256,256]{1,0:T(8,128)(2,1)S(1)}, bf16[256,256]{1,0:T(8,128)(2,1)S(1)}, u32[]{:S(2)}, u32[]{:S(2)}) %collective-permute-start.13) | collective-permute-done | bytes 131104 | tf_op jit(solution)/shard_map/ppermute | solution.py:87
  39.8 2.3 %shard_map.250 = (bf16[512,64]{1,0:T(8,128)(2,1)S(1)}, bf16[512,64]{1,0:T(8,128)(2,1)S(1)}, bf16[512,64]{1,0:T(8,128)(2,1)S(1)}, f32[512,1]{1,0:T(8,128)S(1)}, b...) custom-call(s32[2]{0:T(128)S(1)} %pad_add_fusion.place.place_ref, ...), custom_call_target="tpu_custom_call" | custom-call | flops 2147483648 | bytes 3936256 | tf_op jit(solution)/shard_map/pallas_call | solution.py:898
  42.2 1.9 collective-permute-done.15.recv
  44.8 1.3 collective-permute-start.16
  46.2 1.8 shard_map.246
  47.9 3.4 %collective-permute-start.3 = (bf16[640,256]{1,0:T(8,128)(2,1)S(1)}, bf16[640,256]{1,0:T(8,128)(2,1)S(1)}, u32[]{:S(2)}, u32[]{:S(2)}) collective-permute-start(bf16[640,256]{1,0:T(8,128)(2,1)S(1)} %get-tuple-element.105), channel_id=1, source_target_pairs={{0,1},{1,2},{2,3},{3,0},{4,5},{5,6},{6,7},{7,4},{8,9},{9,10},{10,1... | collective-permute-start | bytes 983048 | tf_op jit(solution)/shard_map/ppermute | solution.py:87
  52.2 1.5 collective-permute-start.5
  54.4 2.8 %collective-permute-start.17 = (bf16[32,1024]{1,0:T(8,128)(2,1)S(1)}, bf16[32,1024]{1,0:T(8,128)(2,1)S(1)}, u32[]{:S(2)}, u32[]{:S(2)}) collective-permute-start(bf16[32,1024]{1,0:T(8,128)(2,1)S(1)} %get-tuple-element.120), channel_id=1, source_target_pairs={{0,1},{1,2},{2,3},{3,0},{4,5},{5,6},{6,7},{7,4},{8,9},{9,10},{10,1... | collective-permute-start | bytes 196616 | tf_op jit(solution)/shard_map/ppermute | solution.py:87
  58.1 17.6 %collective-permute-done.17.refs_0_ = bf16[32,1024]{1,0:T(8,128)(2,1)S(1)} collective-permute-done((bf16[32,1024]{1,0:T(8,128)(2,1)S(1)}, bf16[32,1024]{1,0:T(8,128)(2,1)S(1)}, u32[]{:S(2)}, u32[]{:S(2)}) %collective-permute-start.17) | collective-permute-done | bytes 65568 | tf_op jit(solution)/shard_map/ppermute | solution.py:87
  75.8 9.1 %collective-permute-done.18.refs_1_ = bf16[32,1024]{1,0:T(8,128)(2,1)S(1)} collective-permute-done((bf16[32,1024]{1,0:T(8,128)(2,1)S(1)}, bf16[32,1024]{1,0:T(8,128)(2,1)S(1)}, u32[]{:S(2)}, u32[]{:S(2)}) %collective-permute-start.18) | collective-permute-done | bytes 65568 | tf_op jit(solution)/shard_map/ppermute | solution.py:87
  84.8 2.0 collective-permute-done.19.refs_2_
  87.5 2.5 %collective-permute-start.20 = (bf16[32,1024]{1,0:T(8,128)(2,1)S(1)}, bf16[32,1024]{1,0:T(8,128)(2,1)S(1)}, u32[]{:S(2)}, u32[]{:S(2)}) collective-permute-start(bf16[32,1024]{1,0:T(8,128)(2,1)S(1)} %get-tuple-element.125.refs_0_), channel_id=1, source_target_pairs={{0,1},{1,2},{2,3},{3,0},{4,5},{5,6},{6,7},{7,4},{8,9},{9,10},{10,1... | collective-permute-start | bytes 196616 | tf_op jit(solution)/shard_map/ppermute | solution.py:87
  90.0 1.5 collective-permute-start.21
  91.6 2.8 %collective-permute-start.22 = (bf16[32,1024]{1,0:T(8,128)(2,1)S(1)}, bf16[32,1024]{1,0:T(8,128)(2,1)S(1)}, u32[]{:S(2)}, u32[]{:S(2)}) collective-permute-start(bf16[32,1024]{1,0:T(8,128)(2,1)S(1)} %get-tuple-element.125.refs_0_), channel_id=1, source_target_pairs={{0,3},{1,0},{2,1},{3,2},{4,7},{5,4},{6,5},{7,6},{8,11},{9,8},{10,9... | collective-permute-start | bytes 196616 | tf_op jit(solution)/shard_map/ppermute | solution.py:87
  97.9 4.6 %collective-permute-done.6.refs_1_.refs_5_ = bf16[128,1024]{1,0:T(8,128)(2,1)S(1)} collective-permute-done((bf16[128,1024]{1,0:T(8,128)(2,1)S(1)}, bf16[128,1024]{1,0:T(8,128)(2,1)S(1)}, u32[]{:S(2)}, u32[]{:S(2)}) %collective-permute-start.6) | collective-permute-done | bytes 262176 | tf_op jit(solution)/shard_map/ppermute | solution.py:92
  103.0 2.3 %collective-permute-done.23.refs_1_ = bf16[128,1024]{1,0:T(8,128)(2,1)S(1)} collective-permute-done((bf16[128,1024]{1,0:T(8,128)(2,1)S(1)}, bf16[128,1024]{1,0:T(8,128)(2,1)S(1)}, u32[]{:S(2)}, u32[]{:S(2)}) %collective-permute-start.23) | collective-permute-done | bytes 262176 | tf_op jit(solution)/shard_map/ppermute | solution.py:92
  105.3 1.3 shard_map.248.cot_down
  106.8 1.6 shard_map.255
  108.9 1.5 collective-permute-done.31.recv
  111.8 7.9 %collective-permute-done.32.recv = bf16[128,1024]{1,0:T(8,128)(2,1)S(1)} collective-permute-done((bf16[128,1024]{1,0:T(8,128)(2,1)S(1)}, bf16[128,1024]{1,0:T(8,128)(2,1)S(1)}, u32[]{:S(2)}, u32[]{:S(2)}) %collective-permute-start.32) | collective-permute-done | bytes 262176 | tf_op jit(solution)/shard_map/ppermute | solution.py:92
  121.0 2.1 collective-permute-start.34
  124.2 2.9 %collective-permute-done.33.refs_0_ = bf16[32,1024]{1,0:T(8,128)(2,1)S(1)} collective-permute-done((bf16[32,1024]{1,0:T(8,128)(2,1)S(1)}, bf16[32,1024]{1,0:T(8,128)(2,1)S(1)}, u32[]{:S(2)}, u32[]{:S(2)}) %collective-permute-start.33) | collective-permute-done | bytes 65568 | tf_op jit(solution)/shard_map/ppermute | solution.py:87
  127.1 1.4 collective-permute-done.34.refs_1_
  129.3 1.4 collective-permute-start.36
  130.7 1.7 collective-permute-start.37
  133.2 2.9 %collective-permute-done.36.refs_1_ = bf16[32,1024]{1,0:T(8,128)(2,1)S(1)} collective-permute-done((bf16[32,1024]{1,0:T(8,128)(2,1)S(1)}, bf16[32,1024]{1,0:T(8,128)(2,1)S(1)}, u32[]{:S(2)}, u32[]{:S(2)}) %collective-permute-start.36) | collective-permute-done | bytes 65568 | tf_op jit(solution)/shard_map/ppermute | solution.py:87
  136.1 1.3 collective-permute-done.37.refs_2_
  138.7 1.8 shard_map.272.mine
  140.6 1.4 collective-permute-start.54
  142.0 3.3 %collective-permute-done.39.refs_1_.refs_5_ = bf16[128,1024]{1,0:T(8,128)(2,1)S(1)} collective-permute-done((bf16[128,1024]{1,0:T(8,128)(2,1)S(1)}, bf16[128,1024]{1,0:T(8,128)(2,1)S(1)}, u32[]{:S(2)}, u32[]{:S(2)}) %collective-permute-start.39) | collective-permute-done | bytes 262176 | tf_op jit(solution)/shard_map/ppermute | solution.py:92
  146.9 1.2 shard_map.260.probs
  148.1 2.5 %shard_map.265 = (bf16[512,192]{1,0:T(8,128)(2,1)S(1)}, f32[1,128]{1,0:T(1,128)S(1)}, f32[256,1024]{1,0:T(8,128)S(1)}, bf16[256,1024]{1,0:T(8,128)(2,1)S(1)}) custom-call(s32[2]{0:T(128)S(1)} %pad_add_fusion.place.place_ref, bf16[1024,192]{1,0:T(8,128)(2,1)S(1)} %get-tuple-element.138.wq, bf16[1024,64]{1,0:T(8,128)(2,1)S(1)} %get-tuple-element.139.wo, ...), custom_call_target="tpu_custom_call" | custom-call | bytes 4653568 | tf_op jit(solution)/shard_map/pallas_call | solution.py:33
  150.7 1.6 shard_map.269.mine
  152.3 1.6 collective-permute-start.50
  155.8 1.5 collective-permute-start.43
  157.3 6.4 %collective-permute-done.27.recv = bf16[128,1024]{1,0:T(8,128)(2,1)S(1)} collective-permute-done((bf16[128,1024]{1,0:T(8,128)(2,1)S(1)}, bf16[128,1024]{1,0:T(8,128)(2,1)S(1)}, u32[]{:S(2)}, u32[]{:S(2)}) %collective-permute-start.27) | collective-permute-done | bytes 262176 | tf_op jit(solution)/shard_map/ppermute | solution.py:92
  165.5 1.4 collective-permute-done.54.other
  167.7 1.3 collective-permute-start.55
  170.5 2.5 %collective-permute-start.45 = (bf16[144,256]{1,0:T(8,128)(2,1)S(1)}, bf16[144,256]{1,0:T(8,128)(2,1)S(1)}, u32[]{:S(2)}, u32[]{:S(2)}) collective-permute-start(bf16[144,256]{1,0:T(8,128)(2,1)S(1)} %get-tuple-element.164), channel_id=1, source_target_pairs={{0,2},{1,3},{2,0},{3,1},{4,6},{5,7},{6,4},{7,5},{8,10},{9,11},{10,... | collective-permute-start | bytes 221192 | tf_op jit(solution)/shard_map/ppermute | solution.py:87
  173.0 2.0 collective-permute-start.46
  175.0 4.9 %collective-permute-done.44.refs_0_ = bf16[144,256]{1,0:T(8,128)(2,1)S(1)} collective-permute-done((bf16[144,256]{1,0:T(8,128)(2,1)S(1)}, bf16[144,256]{1,0:T(8,128)(2,1)S(1)}, u32[]{:S(2)}, u32[]{:S(2)}) %collective-permute-start.44) | collective-permute-done | bytes 73760 | tf_op jit(solution)/shard_map/ppermute | solution.py:87
  179.9 2.1 collective-permute-start.29
  181.9 3.2 %collective-permute-done.45.refs_1_ = bf16[144,256]{1,0:T(8,128)(2,1)S(1)} collective-permute-done((bf16[144,256]{1,0:T(8,128)(2,1)S(1)}, bf16[144,256]{1,0:T(8,128)(2,1)S(1)}, u32[]{:S(2)}, u32[]{:S(2)}) %collective-permute-start.45) | collective-permute-done | bytes 73760 | tf_op jit(solution)/shard_map/ppermute | solution.py:87
  185.1 1.4 shard_map.268
  186.5 4.4 %collective-permute-done.29.refs_1_ = bf16[128,256]{1,0:T(8,128)(2,1)S(1)} collective-permute-done((bf16[128,256]{1,0:T(8,128)(2,1)S(1)}, bf16[128,256]{1,0:T(8,128)(2,1)S(1)}, u32[]{:S(2)}, u32[]{:S(2)}) %collective-permute-start.29) | collective-permute-done | bytes 65568 | tf_op jit(solution)/shard_map/ppermute | solution.py:87
  191.0 1.2 collective-permute-done.47
  193.8 10.1 %collective-permute-done.30.refs_2_ = bf16[128,256]{1,0:T(8,128)(2,1)S(1)} collective-permute-done((bf16[128,256]{1,0:T(8,128)(2,1)S(1)}, bf16[128,256]{1,0:T(8,128)(2,1)S(1)}, u32[]{:S(2)}, u32[]{:S(2)}) %collective-permute-start.30) | collective-permute-done | bytes 65568 | tf_op jit(solution)/shard_map/ppermute | solution.py:87
  204.5 3.3 %collective-permute-start.53 = (bf16[272,256]{1,0:T(8,128)(2,1)S(1)}, bf16[272,256]{1,0:T(8,128)(2,1)S(1)}, u32[]{:S(2)}, u32[]{:S(2)}) collective-permute-start(bf16[272,256]{1,0:T(8,128)(2,1)S(1)} %get-tuple-element.173), channel_id=1, source_target_pairs={{0,3},{1,0},{2,1},{3,2},{4,7},{5,4},{6,5},{7,6},{8,11},{9,8},{10,9... | collective-permute-start | bytes 417800 | tf_op jit(solution)/shard_map/ppermute | solution.py:87
  207.8 1.2 shard_map.259
  209.0 2.0 shard_map.274
  211.0 1.3 collective-permute-done.51.refs_1_
  212.4 5.0 %collective-permute-done.52.refs_2_ = bf16[272,256]{1,0:T(8,128)(2,1)S(1)} collective-permute-done((bf16[272,256]{1,0:T(8,128)(2,1)S(1)}, bf16[272,256]{1,0:T(8,128)(2,1)S(1)}, u32[]{:S(2)}, u32[]{:S(2)}) %collective-permute-start.52) | collective-permute-done | bytes 139296 | tf_op jit(solution)/shard_map/ppermute | solution.py:87
  217.4 2.2 %shard_map.271 = (f32[256,768]{1,0:T(8,128)}, f32[256,256]{1,0:T(8,128)}, f32[1,512]{1,0:T(1,128)}) custom-call(s32[2]{0:T(128)S(1)} %pad_add_fusion.place.place_ref, f32[272,256]{1,0:T(8,128)S(1)} %get-tuple-element.170.refs_0_, bf16[272,256]{1,0:T(8,128)(2,1)S(1)} %collective-permute-done.51.refs_1_, bf16[272,256]{1,0:T(8,128)(2,1)S(1)} %collective-permute-done.52.refs_2_, ...), custom_call_target="tpu_custom_call" | custom-call | bytes 1746944 | tf_op jit(solution)/shard_map/pallas_call | solution.py:33
  (109 shorter events, 31.5 us)
Async XLA Ops:
  2.3 7.8 %collective-permute-start = (bf16[144,256]{1,0:T(8,128)(2,1)S(1)}, bf16[144,256]{1,0:T(8,128)(2,1)S(1)}, u32[]{:S(2)}, u32[]{:S(2)}) collective-permute-start(bf16[144,256]{1,0:T(8,128)(2,1)S(1)} %head.1.refs_0_), channel_id=1, source_target_pairs={{0,1},{1,2},{2,3},{3,0},{4,5},{5,6},{6,7},{7,4},{8,9},{9,10},{10,1... | collective-permute-start | bytes 221192 | tf_op jit(solution)/shard_map/ppermute | solution.py:87
  5.4 7.5 %collective-permute-start.1 = (bf16[144,256]{1,0:T(8,128)(2,1)S(1)}, bf16[144,256]{1,0:T(8,128)(2,1)S(1)}, u32[]{:S(2)}, u32[]{:S(2)}) collective-permute-start(bf16[144,256]{1,0:T(8,128)(2,1)S(1)} %head.1.refs_0_), channel_id=1, source_target_pairs={{0,2},{1,3},{2,0},{3,1},{4,6},{5,7},{6,4},{7,5},{8,10},{9,11},{10,... | collective-permute-start | bytes 221192 | tf_op jit(solution)/shard_map/ppermute | solution.py:87
  8.0 5.2 %collective-permute-start.2 = (bf16[144,256]{1,0:T(8,128)(2,1)S(1)}, bf16[144,256]{1,0:T(8,128)(2,1)S(1)}, u32[]{:S(2)}, u32[]{:S(2)}) collective-permute-start(bf16[144,256]{1,0:T(8,128)(2,1)S(1)} %head.1.refs_0_), channel_id=1, source_target_pairs={{0,3},{1,0},{2,1},{3,2},{4,7},{5,4},{6,5},{7,6},{8,11},{9,8},{10,9... | collective-permute-start | bytes 221192 | tf_op jit(solution)/shard_map/ppermute | solution.py:87
  14.0 8.0 %collective-permute-start.9 = (bf16[128,1024]{1,0:T(8,128)(2,1)S(1)}, bf16[128,1024]{1,0:T(8,128)(2,1)S(1)}, u32[]{:S(2)}, u32[]{:S(2)}) collective-permute-start(bf16[128,1024]{1,0:T(8,128)(2,1)S(1)} %get-tuple-element.100.refs_1_.refs_0_), channel_id=1, source_target_pairs={{0,8},{4,12},{8,0},{12,4},{1,9},{5,13},{9,1},{13,5},{2,10},{6,14},... | collective-permute-start | bytes 786440 | tf_op jit(solution)/shard_map/ppermute | solution.py:92
  15.5 23.6 %collective-permute-start.10 = (bf16[128,1024]{1,0:T(8,128)(2,1)S(1)}, bf16[128,1024]{1,0:T(8,128)(2,1)S(1)}, u32[]{:S(2)}, u32[]{:S(2)}) collective-permute-start(bf16[128,1024]{1,0:T(8,128)(2,1)S(1)} %get-tuple-element.100.refs_1_.refs_0_), channel_id=1, source_target_pairs={{0,4},{4,0},{8,12},{12,8},{1,5},{5,1},{9,13},{13,9},{2,6},{6,2},{1... | collective-permute-start | bytes 786440 | tf_op jit(solution)/shard_map/ppermute | solution.py:92
  21.9 17.2 %collective-permute-start.11 = (bf16[128,1024]{1,0:T(8,128)(2,1)S(1)}, bf16[128,1024]{1,0:T(8,128)(2,1)S(1)}, u32[]{:S(2)}, u32[]{:S(2)}) collective-permute-start(bf16[128,1024]{1,0:T(8,128)(2,1)S(1)} %collective-permute-done.9.refs_2_.refs_1_), channel_id=1, source_target_pairs={{0,4},{4,0},{8,12},{12,8},{1,5},{5,1},{9,13},{13,9},{2,6},{6,2},{1... | collective-permute-start | bytes 786440 | tf_op jit(solution)/shard_map/ppermute | solution.py:92
  21.9 1.0 copy-start.2
  25.7 8.3 %collective-permute-start.12 = (bf16[256,256]{1,0:T(8,128)(2,1)S(1)}, bf16[256,256]{1,0:T(8,128)(2,1)S(1)}, u32[]{:S(2)}, u32[]{:S(2)}) collective-permute-start(bf16[256,256]{1,0:T(8,128)(2,1)S(1)} %get-tuple-element.112), channel_id=1, source_target_pairs={{0,1},{1,2},{2,3},{3,0},{4,5},{5,6},{6,7},{7,4},{8,9},{9,10},{10,1... | collective-permute-start | bytes 393224 | tf_op jit(solution)/shard_map/ppermute | solution.py:87
  27.9 11.3 %collective-permute-start.13 = (bf16[256,256]{1,0:T(8,128)(2,1)S(1)}, bf16[256,256]{1,0:T(8,128)(2,1)S(1)}, u32[]{:S(2)}, u32[]{:S(2)}) collective-permute-start(bf16[256,256]{1,0:T(8,128)(2,1)S(1)} %get-tuple-element.113), channel_id=1, source_target_pairs={{0,2},{1,3},{2,0},{3,1},{4,6},{5,7},{6,4},{7,5},{8,10},{9,11},{10,... | collective-permute-start | bytes 393224 | tf_op jit(solution)/shard_map/ppermute | solution.py:87
  29.0 10.1 %collective-permute-start.14 = (bf16[256,256]{1,0:T(8,128)(2,1)S(1)}, bf16[256,256]{1,0:T(8,128)(2,1)S(1)}, u32[]{:S(2)}, u32[]{:S(2)}) collective-permute-start(bf16[256,256]{1,0:T(8,128)(2,1)S(1)} %get-tuple-element.114), channel_id=1, source_target_pairs={{0,3},{1,0},{2,1},{3,2},{4,7},{5,4},{6,5},{7,6},{8,11},{9,8},{10,9... | collective-permute-start | bytes 393224 | tf_op jit(solution)/shard_map/ppermute | solution.py:87
  42.1 4.0 %copy-start = (bf16[256,1024]{1,0:T(8,128)(2,1)S(1)}, bf16[256,1024]{1,0:T(8,128)(2,1)}, u32[]{:S(2)}) copy-start(bf16[256,1024]{1,0:T(8,128)(2,1)} %w_up) | copy-start | bytes 1572868
  42.1 4.0 %copy-start.1 = (bf16[1024,256]{1,0:T(8,128)(2,1)S(1)}, bf16[1024,256]{1,0:T(8,128)(2,1)}, u32[]{:S(2)}) copy-start(bf16[1024,256]{1,0:T(8,128)(2,1)} %w_down) | copy-start | bytes 1572868
  42.1 4.0 %copy-start.4 = (bf16[128,256]{1,0:T(8,128)(2,1)S(1)}, bf16[128,256]{1,0:T(8,128)(2,1)}, u32[]{:S(2)}) copy-start(bf16[128,256]{1,0:T(8,128)(2,1)} %cotangent) | copy-start | bytes 196612
  42.2 2.0 collective-permute-start.15
  44.8 8.9 %collective-permute-start.16 = (bf16[128,1024]{1,0:T(8,128)(2,1)S(1)}, bf16[128,1024]{1,0:T(8,128)(2,1)S(1)}, u32[]{:S(2)}, u32[]{:S(2)}) collective-permute-start(bf16[128,1024]{1,0:T(8,128)(2,1)S(1)} %get-tuple-element.118), channel_id=1, source_target_pairs={{0,8},{4,12},{8,0},{12,4},{1,9},{5,13},{9,1},{13,5},{2,10},{6,14},... | collective-permute-start | bytes 786440 | tf_op jit(solution)/shard_map/ppermute | solution.py:92
  47.9 43.7 %collective-permute-start.3 = (bf16[640,256]{1,0:T(8,128)(2,1)S(1)}, bf16[640,256]{1,0:T(8,128)(2,1)S(1)}, u32[]{:S(2)}, u32[]{:S(2)}) collective-permute-start(bf16[640,256]{1,0:T(8,128)(2,1)S(1)} %get-tuple-element.105), channel_id=1, source_target_pairs={{0,1},{1,2},{2,3},{3,0},{4,5},{5,6},{6,7},{7,4},{8,9},{9,10},{10,1... | collective-permute-start | bytes 983048 | tf_op jit(solution)/shard_map/ppermute | solution.py:87
  51.3 43.1 %collective-permute-start.4 = (bf16[640,256]{1,0:T(8,128)(2,1)S(1)}, bf16[640,256]{1,0:T(8,128)(2,1)S(1)}, u32[]{:S(2)}, u32[]{:S(2)}) collective-permute-start(bf16[640,256]{1,0:T(8,128)(2,1)S(1)} %get-tuple-element.106), channel_id=1, source_target_pairs={{0,2},{1,3},{2,0},{3,1},{4,6},{5,7},{6,4},{7,5},{8,10},{9,11},{10,... | collective-permute-start | bytes 983048 | tf_op jit(solution)/shard_map/ppermute | solution.py:87
  52.2 42.2 %collective-permute-start.5 = (bf16[640,256]{1,0:T(8,128)(2,1)S(1)}, bf16[640,256]{1,0:T(8,128)(2,1)S(1)}, u32[]{:S(2)}, u32[]{:S(2)}) collective-permute-start(bf16[640,256]{1,0:T(8,128)(2,1)S(1)} %get-tuple-element.107), channel_id=1, source_target_pairs={{0,3},{1,0},{2,1},{3,2},{4,7},{5,4},{6,5},{7,6},{8,11},{9,8},{10,9... | collective-permute-start | bytes 983048 | tf_op jit(solution)/shard_map/ppermute | solution.py:87
  54.4 21.4 %collective-permute-start.17 = (bf16[32,1024]{1,0:T(8,128)(2,1)S(1)}, bf16[32,1024]{1,0:T(8,128)(2,1)S(1)}, u32[]{:S(2)}, u32[]{:S(2)}) collective-permute-start(bf16[32,1024]{1,0:T(8,128)(2,1)S(1)} %get-tuple-element.120), channel_id=1, source_target_pairs={{0,1},{1,2},{2,3},{3,0},{4,5},{5,6},{6,7},{7,4},{8,9},{9,10},{10,1... | collective-permute-start | bytes 196616 | tf_op jit(solution)/shard_map/ppermute | solution.py:87
  57.2 27.7 %collective-permute-start.18 = (bf16[32,1024]{1,0:T(8,128)(2,1)S(1)}, bf16[32,1024]{1,0:T(8,128)(2,1)S(1)}, u32[]{:S(2)}, u32[]{:S(2)}) collective-permute-start(bf16[32,1024]{1,0:T(8,128)(2,1)S(1)} %get-tuple-element.121), channel_id=1, source_target_pairs={{0,2},{1,3},{2,0},{3,1},{4,6},{5,7},{6,4},{7,5},{8,10},{9,11},{10,... | collective-permute-start | bytes 196616 | tf_op jit(solution)/shard_map/ppermute | solution.py:87
  75.7 11.1 %collective-permute-start.19 = (bf16[32,1024]{1,0:T(8,128)(2,1)S(1)}, bf16[32,1024]{1,0:T(8,128)(2,1)S(1)}, u32[]{:S(2)}, u32[]{:S(2)}) collective-permute-start(bf16[32,1024]{1,0:T(8,128)(2,1)S(1)} %get-tuple-element.122), channel_id=1, source_target_pairs={{0,3},{1,0},{2,1},{3,2},{4,7},{5,4},{6,5},{7,6},{8,11},{9,8},{10,9... | collective-permute-start | bytes 196616 | tf_op jit(solution)/shard_map/ppermute | solution.py:87
  87.5 8.4 %collective-permute-start.20 = (bf16[32,1024]{1,0:T(8,128)(2,1)S(1)}, bf16[32,1024]{1,0:T(8,128)(2,1)S(1)}, u32[]{:S(2)}, u32[]{:S(2)}) collective-permute-start(bf16[32,1024]{1,0:T(8,128)(2,1)S(1)} %get-tuple-element.125.refs_0_), channel_id=1, source_target_pairs={{0,1},{1,2},{2,3},{3,0},{4,5},{5,6},{6,7},{7,4},{8,9},{9,10},{10,1... | collective-permute-start | bytes 196616 | tf_op jit(solution)/shard_map/ppermute | solution.py:87
  90.0 5.8 %collective-permute-start.21 = (bf16[32,1024]{1,0:T(8,128)(2,1)S(1)}, bf16[32,1024]{1,0:T(8,128)(2,1)S(1)}, u32[]{:S(2)}, u32[]{:S(2)}) collective-permute-start(bf16[32,1024]{1,0:T(8,128)(2,1)S(1)} %get-tuple-element.125.refs_0_), channel_id=1, source_target_pairs={{0,2},{1,3},{2,0},{3,1},{4,6},{5,7},{6,4},{7,5},{8,10},{9,11},{10,... | collective-permute-start | bytes 196616 | tf_op jit(solution)/shard_map/ppermute | solution.py:87
  91.6 4.8 %collective-permute-start.22 = (bf16[32,1024]{1,0:T(8,128)(2,1)S(1)}, bf16[32,1024]{1,0:T(8,128)(2,1)S(1)}, u32[]{:S(2)}, u32[]{:S(2)}) collective-permute-start(bf16[32,1024]{1,0:T(8,128)(2,1)S(1)} %get-tuple-element.125.refs_0_), channel_id=1, source_target_pairs={{0,3},{1,0},{2,1},{3,2},{4,7},{5,4},{6,5},{7,6},{8,11},{9,8},{10,9... | collective-permute-start | bytes 196616 | tf_op jit(solution)/shard_map/ppermute | solution.py:87
  95.1 7.4 %collective-permute-start.6 = (bf16[128,1024]{1,0:T(8,128)(2,1)S(1)}, bf16[128,1024]{1,0:T(8,128)(2,1)S(1)}, u32[]{:S(2)}, u32[]{:S(2)}) collective-permute-start(bf16[128,1024]{1,0:T(8,128)(2,1)S(1)} %get-tuple-element.110.refs_0_.refs_6_.refs_4_), channel_id=1, source_target_pairs={{0,8},{4,12},{8,0},{12,4},{1,9},{5,13},{9,1},{13,5},{2,10},{6,14},... | collective-permute-start | bytes 786440 | tf_op jit(solution)/shard_map/ppermute | solution.py:92
  96.9 9.9 %copy-start.6 = (f32[1024]{0:T(1024)S(1)}, f32[1024]{0:T(1024)}, u32[]{:S(2)}) copy-start(f32[1024]{0:T(1024)} %param.25) | copy-start | bytes 12292
  96.9 8.4 %collective-permute-start.23 = (bf16[128,1024]{1,0:T(8,128)(2,1)S(1)}, bf16[128,1024]{1,0:T(8,128)(2,1)S(1)}, u32[]{:S(2)}, u32[]{:S(2)}) collective-permute-start(bf16[128,1024]{1,0:T(8,128)(2,1)S(1)} %shard_map.254.refs_0_), channel_id=1, source_target_pairs={{0,8},{4,12},{8,0},{12,4},{1,9},{5,13},{9,1},{13,5},{2,10},{6,14},... | collective-permute-start | bytes 786440 | tf_op jit(solution)/shard_map/ppermute | solution.py:92
  97.9 7.4 %collective-permute-start.7 = (bf16[128,1024]{1,0:T(8,128)(2,1)S(1)}, bf16[128,1024]{1,0:T(8,128)(2,1)S(1)}, u32[]{:S(2)}, u32[]{:S(2)}) collective-permute-start(bf16[128,1024]{1,0:T(8,128)(2,1)S(1)} %get-tuple-element.110.refs_0_.refs_6_.refs_4_), channel_id=1, source_target_pairs={{0,4},{4,0},{8,12},{12,8},{1,5},{5,1},{9,13},{13,9},{2,6},{6,2},{1... | collective-permute-start | bytes 786440 | tf_op jit(solution)/shard_map/ppermute | solution.py:92
  102.5 2.8 %collective-permute-start.8 = (bf16[128,1024]{1,0:T(8,128)(2,1)S(1)}, bf16[128,1024]{1,0:T(8,128)(2,1)S(1)}, u32[]{:S(2)}, u32[]{:S(2)}) collective-permute-start(bf16[128,1024]{1,0:T(8,128)(2,1)S(1)} %collective-permute-done.6.refs_1_.refs_5_), channel_id=1, source_target_pairs={{0,4},{4,0},{8,12},{12,8},{1,5},{5,1},{9,13},{13,9},{2,6},{6,2},{1... | collective-permute-start | bytes 786440 | tf_op jit(solution)/shard_map/ppermute | solution.py:92
  102.5 4.2 %collective-permute-start.24 = (bf16[128,1024]{1,0:T(8,128)(2,1)S(1)}, bf16[128,1024]{1,0:T(8,128)(2,1)S(1)}, u32[]{:S(2)}, u32[]{:S(2)}) collective-permute-start(bf16[128,1024]{1,0:T(8,128)(2,1)S(1)} %shard_map.254.refs_0_), channel_id=1, source_target_pairs={{0,4},{4,0},{8,12},{12,8},{1,5},{5,1},{9,13},{13,9},{2,6},{6,2},{1... | collective-permute-start | bytes 786440 | tf_op jit(solution)/shard_map/ppermute | solution.py:92
  105.3 1.5 collective-permute-start.25
  108.4 2.0 collective-permute-start.31
  111.1 8.6 %collective-permute-start.32 = (bf16[128,1024]{1,0:T(8,128)(2,1)S(1)}, bf16[128,1024]{1,0:T(8,128)(2,1)S(1)}, u32[]{:S(2)}, u32[]{:S(2)}) collective-permute-start(bf16[128,1024]{1,0:T(8,128)(2,1)S(1)} %get-tuple-element.148), channel_id=1, source_target_pairs={{0,8},{4,12},{8,0},{12,4},{1,9},{5,13},{9,1},{13,5},{2,10},{6,14},... | collective-permute-start | bytes 786440 | tf_op jit(solution)/shard_map/ppermute | solution.py:92
  120.3 6.8 %collective-permute-start.33 = (bf16[32,1024]{1,0:T(8,128)(2,1)S(1)}, bf16[32,1024]{1,0:T(8,128)(2,1)S(1)}, u32[]{:S(2)}, u32[]{:S(2)}) collective-permute-start(bf16[32,1024]{1,0:T(8,128)(2,1)S(1)} %get-tuple-element.150), channel_id=1, source_target_pairs={{0,1},{1,2},{2,3},{3,0},{4,5},{5,6},{6,7},{7,4},{8,9},{9,10},{10,1... | collective-permute-start | bytes 196616 | tf_op jit(solution)/shard_map/ppermute | solution.py:87
  121.0 7.6 %collective-permute-start.34 = (bf16[32,1024]{1,0:T(8,128)(2,1)S(1)}, bf16[32,1024]{1,0:T(8,128)(2,1)S(1)}, u32[]{:S(2)}, u32[]{:S(2)}) collective-permute-start(bf16[32,1024]{1,0:T(8,128)(2,1)S(1)} %get-tuple-element.151), channel_id=1, source_target_pairs={{0,2},{1,3},{2,0},{3,1},{4,6},{5,7},{6,4},{7,5},{8,10},{9,11},{10,... | collective-permute-start | bytes 196616 | tf_op jit(solution)/shard_map/ppermute | solution.py:87
  123.2 5.4 %collective-permute-start.35 = (bf16[32,1024]{1,0:T(8,128)(2,1)S(1)}, bf16[32,1024]{1,0:T(8,128)(2,1)S(1)}, u32[]{:S(2)}, u32[]{:S(2)}) collective-permute-start(bf16[32,1024]{1,0:T(8,128)(2,1)S(1)} %get-tuple-element.152), channel_id=1, source_target_pairs={{0,3},{1,0},{2,1},{3,2},{4,7},{5,4},{6,5},{7,6},{8,11},{9,8},{10,9... | collective-permute-start | bytes 196616 | tf_op jit(solution)/shard_map/ppermute | solution.py:87
  129.3 6.8 %collective-permute-start.36 = (bf16[32,1024]{1,0:T(8,128)(2,1)S(1)}, bf16[32,1024]{1,0:T(8,128)(2,1)S(1)}, u32[]{:S(2)}, u32[]{:S(2)}) collective-permute-start(bf16[32,1024]{1,0:T(8,128)(2,1)S(1)} %get-tuple-element.155.refs_0_), channel_id=1, source_target_pairs={{0,1},{1,2},{2,3},{3,0},{4,5},{5,6},{6,7},{7,4},{8,9},{9,10},{10,1... | collective-permute-start | bytes 196616 | tf_op jit(solution)/shard_map/ppermute | solution.py:87
  130.7 6.7 %collective-permute-start.37 = (bf16[32,1024]{1,0:T(8,128)(2,1)S(1)}, bf16[32,1024]{1,0:T(8,128)(2,1)S(1)}, u32[]{:S(2)}, u32[]{:S(2)}) collective-permute-start(bf16[32,1024]{1,0:T(8,128)(2,1)S(1)} %get-tuple-element.155.refs_0_), channel_id=1, source_target_pairs={{0,2},{1,3},{2,0},{3,1},{4,6},{5,7},{6,4},{7,5},{8,10},{9,11},{10,... | collective-permute-start | bytes 196616 | tf_op jit(solution)/shard_map/ppermute | solution.py:87
  132.4 5.0 %collective-permute-start.38 = (bf16[32,1024]{1,0:T(8,128)(2,1)S(1)}, bf16[32,1024]{1,0:T(8,128)(2,1)S(1)}, u32[]{:S(2)}, u32[]{:S(2)}) collective-permute-start(bf16[32,1024]{1,0:T(8,128)(2,1)S(1)} %get-tuple-element.155.refs_0_), channel_id=1, source_target_pairs={{0,3},{1,0},{2,1},{3,2},{4,7},{5,4},{6,5},{7,6},{8,11},{9,8},{10,9... | collective-permute-start | bytes 196616 | tf_op jit(solution)/shard_map/ppermute | solution.py:87
  138.0 7.3 %collective-permute-start.39 = (bf16[128,1024]{1,0:T(8,128)(2,1)S(1)}, bf16[128,1024]{1,0:T(8,128)(2,1)S(1)}, u32[]{:S(2)}, u32[]{:S(2)}) collective-permute-start(bf16[128,1024]{1,0:T(8,128)(2,1)S(1)} %shard_map.264.refs_0_.refs_4_), channel_id=1, source_target_pairs={{0,8},{4,12},{8,0},{12,4},{1,9},{5,13},{9,1},{13,5},{2,10},{6,14},... | collective-permute-start | bytes 786440 | tf_op jit(solution)/shard_map/ppermute | solution.py:92
  140.6 26.3 %collective-permute-start.54 = (bf16[2064,256]{1,0:T(8,128)(2,1)S(1)}, bf16[2064,256]{1,0:T(8,128)(2,1)S(1)}, u32[]{:S(2)}, u32[]{:S(2)}) collective-permute-start(bf16[2064,256]{1,0:T(8,128)(2,1)S(1)} %shard_map.272.mine), channel_id=1, source_target_pairs={{0,16},{16,0},{1,17},{17,1},{2,18},{18,2},{3,19},{19,3},{4,20},{20... | collective-permute-start | bytes 3170312 | tf_op jit(solution)/shard_map/ppermute | solution.py:92
  142.0 6.0 %collective-permute-start.40 = (bf16[128,1024]{1,0:T(8,128)(2,1)S(1)}, bf16[128,1024]{1,0:T(8,128)(2,1)S(1)}, u32[]{:S(2)}, u32[]{:S(2)}) collective-permute-start(bf16[128,1024]{1,0:T(8,128)(2,1)S(1)} %shard_map.264.refs_0_.refs_4_), channel_id=1, source_target_pairs={{0,4},{4,0},{8,12},{12,8},{1,5},{5,1},{9,13},{13,9},{2,6},{6,2},{1... | collective-permute-start | bytes 786440 | tf_op jit(solution)/shard_map/ppermute | solution.py:92
  145.3 2.7 %collective-permute-start.41 = (bf16[128,1024]{1,0:T(8,128)(2,1)S(1)}, bf16[128,1024]{1,0:T(8,128)(2,1)S(1)}, u32[]{:S(2)}, u32[]{:S(2)}) collective-permute-start(bf16[128,1024]{1,0:T(8,128)(2,1)S(1)} %collective-permute-done.39.refs_1_.refs_5_), channel_id=1, source_target_pairs={{0,4},{4,0},{8,12},{12,8},{1,5},{5,1},{9,13},{13,9},{2,6},{6,2},{1... | collective-permute-start | bytes 786440 | tf_op jit(solution)/shard_map/ppermute | solution.py:92
  146.3 7.6 %collective-permute-start.26 = (bf16[256,1024]{1,0:T(8,128)(2,1)S(1)}, bf16[256,1024]{1,0:T(8,128)(2,1)S(1)}, u32[]{:S(2)}, u32[]{:S(2)}) collective-permute-start(bf16[256,1024]{1,0:T(8,128)(2,1)S(1)} %get-tuple-element.128), channel_id=1, source_target_pairs={{0,4},{4,0},{8,12},{12,8},{1,5},{5,1},{9,13},{13,9},{2,6},{6,2},{1... | collective-permute-start | bytes 1572872 | tf_op jit(solution)/shard_map/ppermute | solution.py:92
  150.6 4.5 %collective-permute-start.42 = (bf16[256,1024]{1,0:T(8,128)(2,1)S(1)}, bf16[256,1024]{1,0:T(8,128)(2,1)S(1)}, u32[]{:S(2)}, u32[]{:S(2)}) collective-permute-start(bf16[256,1024]{1,0:T(8,128)(2,1)S(1)} %get-tuple-element.157), channel_id=1, source_target_pairs={{0,4},{4,0},{8,12},{12,8},{1,5},{5,1},{9,13},{13,9},{2,6},{6,2},{1... | collective-permute-start | bytes 1572872 | tf_op jit(solution)/shard_map/ppermute | solution.py:92
  152.3 40.8 %collective-permute-start.50 = (bf16[1040,256]{1,0:T(8,128)(2,1)S(1)}, bf16[1040,256]{1,0:T(8,128)(2,1)S(1)}, u32[]{:S(2)}, u32[]{:S(2)}) collective-permute-start(bf16[1040,256]{1,0:T(8,128)(2,1)S(1)} %shard_map.269.mine), channel_id=1, source_target_pairs={{0,16},{16,0},{1,17},{17,1},{2,18},{18,2},{3,19},{19,3},{4,20},{20... | collective-permute-start | bytes 1597448 | tf_op jit(solution)/shard_map/ppermute | solution.py:92
  154.5 9.2 %collective-permute-start.27 = (bf16[128,1024]{1,0:T(8,128)(2,1)S(1)}, bf16[128,1024]{1,0:T(8,128)(2,1)S(1)}, u32[]{:S(2)}, u32[]{:S(2)}) collective-permute-start(bf16[128,1024]{1,0:T(8,128)(2,1)S(1)} %get-tuple-element.130), channel_id=1, source_target_pairs={{0,8},{4,12},{8,0},{12,4},{1,9},{5,13},{9,1},{13,5},{2,10},{6,14},... | collective-permute-start | bytes 786440 | tf_op jit(solution)/shard_map/ppermute | solution.py:92
  155.8 13.2 %collective-permute-start.43 = (bf16[128,1024]{1,0:T(8,128)(2,1)S(1)}, bf16[128,1024]{1,0:T(8,128)(2,1)S(1)}, u32[]{:S(2)}, u32[]{:S(2)}) collective-permute-start(bf16[128,1024]{1,0:T(8,128)(2,1)S(1)} %get-tuple-element.159), channel_id=1, source_target_pairs={{0,8},{4,12},{8,0},{12,4},{1,9},{5,13},{9,1},{13,5},{2,10},{6,14},... | collective-permute-start | bytes 786440 | tf_op jit(solution)/shard_map/ppermute | solution.py:92
  164.4 8.6 %collective-permute-start.28 = (bf16[128,256]{1,0:T(8,128)(2,1)S(1)}, bf16[128,256]{1,0:T(8,128)(2,1)S(1)}, u32[]{:S(2)}, u32[]{:S(2)}) collective-permute-start(bf16[128,256]{1,0:T(8,128)(2,1)S(1)} %get-tuple-element.133), channel_id=1, source_target_pairs={{0,1},{1,2},{2,3},{3,0},{4,5},{5,6},{6,7},{7,4},{8,9},{9,10},{10,1... | collective-permute-start | bytes 196616 | tf_op jit(solution)/shard_map/ppermute | solution.py:87
  167.7 36.8 %collective-permute-start.55 = (bf16[528,256]{1,0:T(8,128)(2,1)S(1)}, bf16[528,256]{1,0:T(8,128)(2,1)S(1)}, u32[]{:S(2)}, u32[]{:S(2)}) collective-permute-start(bf16[528,256]{1,0:T(8,128)(2,1)S(1)} %get-tuple-element.180), channel_id=1, source_target_pairs={{0,1},{1,2},{2,3},{3,0},{4,5},{5,6},{6,7},{7,4},{8,9},{9,10},{10,1... | collective-permute-start | bytes 811016 | tf_op jit(solution)/shard_map/ppermute | solution.py:87
  169.9 37.9 %copy-start.7 = (f32[256]{0:T(256)S(1)}, f32[256]{0:T(256)}, u32[]{:S(2)}) copy-start(f32[256]{0:T(256)} %param.27) | copy-start | bytes 3076
  169.9 10.0 %collective-permute-start.44 = (bf16[144,256]{1,0:T(8,128)(2,1)S(1)}, bf16[144,256]{1,0:T(8,128)(2,1)S(1)}, u32[]{:S(2)}, u32[]{:S(2)}) collective-permute-start(bf16[144,256]{1,0:T(8,128)(2,1)S(1)} %get-tuple-element.163), channel_id=1, source_target_pairs={{0,1},{1,2},{2,3},{3,0},{4,5},{5,6},{6,7},{7,4},{8,9},{9,10},{10,1... | collective-permute-start | bytes 221192 | tf_op jit(solution)/shard_map/ppermute | solution.py:87
  170.5 14.6 %collective-permute-start.45 = (bf16[144,256]{1,0:T(8,128)(2,1)S(1)}, bf16[144,256]{1,0:T(8,128)(2,1)S(1)}, u32[]{:S(2)}, u32[]{:S(2)}) collective-permute-start(bf16[144,256]{1,0:T(8,128)(2,1)S(1)} %get-tuple-element.164), channel_id=1, source_target_pairs={{0,2},{1,3},{2,0},{3,1},{4,6},{5,7},{6,4},{7,5},{8,10},{9,11},{10,... | collective-permute-start | bytes 221192 | tf_op jit(solution)/shard_map/ppermute | solution.py:87
  173.0 12.1 %collective-permute-start.46 = (bf16[144,256]{1,0:T(8,128)(2,1)S(1)}, bf16[144,256]{1,0:T(8,128)(2,1)S(1)}, u32[]{:S(2)}, u32[]{:S(2)}) collective-permute-start(bf16[144,256]{1,0:T(8,128)(2,1)S(1)} %get-tuple-element.165), channel_id=1, source_target_pairs={{0,3},{1,0},{2,1},{3,2},{4,7},{5,4},{6,5},{7,6},{8,11},{9,8},{10,9... | collective-permute-start | bytes 221192 | tf_op jit(solution)/shard_map/ppermute | solution.py:87
  179.9 11.1 %collective-permute-start.29 = (bf16[128,256]{1,0:T(8,128)(2,1)S(1)}, bf16[128,256]{1,0:T(8,128)(2,1)S(1)}, u32[]{:S(2)}, u32[]{:S(2)}) collective-permute-start(bf16[128,256]{1,0:T(8,128)(2,1)S(1)} %get-tuple-element.134), channel_id=1, source_target_pairs={{0,2},{1,3},{2,0},{3,1},{4,6},{5,7},{6,4},{7,5},{8,10},{9,11},{10,... | collective-permute-start | bytes 196616 | tf_op jit(solution)/shard_map/ppermute | solution.py:87
  185.1 22.7 %collective-permute-start.56 = (bf16[528,256]{1,0:T(8,128)(2,1)S(1)}, bf16[528,256]{1,0:T(8,128)(2,1)S(1)}, u32[]{:S(2)}, u32[]{:S(2)}) collective-permute-start(bf16[528,256]{1,0:T(8,128)(2,1)S(1)} %get-tuple-element.181), channel_id=1, source_target_pairs={{0,2},{1,3},{2,0},{3,1},{4,6},{5,7},{6,4},{7,5},{8,10},{9,11},{10,... | collective-permute-start | bytes 811016 | tf_op jit(solution)/shard_map/ppermute | solution.py:87
  185.1 23.9 %collective-permute-start.57 = (bf16[528,256]{1,0:T(8,128)(2,1)S(1)}, bf16[528,256]{1,0:T(8,128)(2,1)S(1)}, u32[]{:S(2)}, u32[]{:S(2)}) collective-permute-start(bf16[528,256]{1,0:T(8,128)(2,1)S(1)} %get-tuple-element.182), channel_id=1, source_target_pairs={{0,3},{1,0},{2,1},{3,2},{4,7},{5,4},{6,5},{7,6},{8,11},{9,8},{10,9... | collective-permute-start | bytes 811016 | tf_op jit(solution)/shard_map/ppermute | solution.py:87
  191.0 1.2 collective-permute-start.47
  192.2 11.7 %collective-permute-start.30 = (bf16[128,256]{1,0:T(8,128)(2,1)S(1)}, bf16[128,256]{1,0:T(8,128)(2,1)S(1)}, u32[]{:S(2)}, u32[]{:S(2)}) collective-permute-start(bf16[128,256]{1,0:T(8,128)(2,1)S(1)} %get-tuple-element.135), channel_id=1, source_target_pairs={{0,3},{1,0},{2,1},{3,2},{4,7},{5,4},{6,5},{7,6},{8,11},{9,8},{10,9... | collective-permute-start | bytes 196616 | tf_op jit(solution)/shard_map/ppermute | solution.py:87
  193.1 11.4 %collective-permute-start.48 = (f32[8,256]{1,0:T(8,128)S(1)}, f32[8,256]{1,0:T(8,128)S(1)}, u32[]{:S(2)}, u32[]{:S(2)}) collective-permute-start(f32[8,256]{1,0:T(8,128)S(1)} %add.19), channel_id=1, source_target_pairs={{0,8},{4,12},{8,0},{12,4},{1,9},{5,13},{9,1},{13,5},{2,10},{6,14},... | collective-permute-start | bytes 24584 | tf_op jit(solution)/shard_map/ppermute | solution.py:92
  203.9 8.5 %collective-permute-start.51 = (bf16[272,256]{1,0:T(8,128)(2,1)S(1)}, bf16[272,256]{1,0:T(8,128)(2,1)S(1)}, u32[]{:S(2)}, u32[]{:S(2)}) collective-permute-start(bf16[272,256]{1,0:T(8,128)(2,1)S(1)} %get-tuple-element.171), channel_id=1, source_target_pairs={{0,1},{1,2},{2,3},{3,0},{4,5},{5,6},{6,7},{7,4},{8,9},{9,10},{10,1... | collective-permute-start | bytes 417800 | tf_op jit(solution)/shard_map/ppermute | solution.py:87
  204.5 12.9 %collective-permute-start.52 = (bf16[272,256]{1,0:T(8,128)(2,1)S(1)}, bf16[272,256]{1,0:T(8,128)(2,1)S(1)}, u32[]{:S(2)}, u32[]{:S(2)}) collective-permute-start(bf16[272,256]{1,0:T(8,128)(2,1)S(1)} %get-tuple-element.172), channel_id=1, source_target_pairs={{0,2},{1,3},{2,0},{3,1},{4,6},{5,7},{6,4},{7,5},{8,10},{9,11},{10,... | collective-permute-start | bytes 417800 | tf_op jit(solution)/shard_map/ppermute | solution.py:87
  204.5 12.9 %collective-permute-start.53 = (bf16[272,256]{1,0:T(8,128)(2,1)S(1)}, bf16[272,256]{1,0:T(8,128)(2,1)S(1)}, u32[]{:S(2)}, u32[]{:S(2)}) collective-permute-start(bf16[272,256]{1,0:T(8,128)(2,1)S(1)} %get-tuple-element.173), channel_id=1, source_target_pairs={{0,3},{1,0},{2,1},{3,2},{4,7},{5,4},{6,5},{7,6},{8,11},{9,8},{10,9... | collective-permute-start | bytes 417800 | tf_op jit(solution)/shard_map/ppermute | solution.py:87
  207.8 11.9 %collective-permute-start.49 = (f32[8,256]{1,0:T(8,128)S(1)}, f32[8,256]{1,0:T(8,128)S(1)}, u32[]{:S(2)}, u32[]{:S(2)}) collective-permute-start(f32[8,256]{1,0:T(8,128)S(1)} %add.20), channel_id=1, source_target_pairs={{0,16},{16,0},{1,17},{17,1},{2,18},{18,2},{3,19},{19,3},{4,20},{20... | collective-permute-start | bytes 24584 | tf_op jit(solution)/shard_map/ppermute | solution.py:92
  (3 other events, 2.4 us)
where the time goes:
time: 221 us; the launch traced here: 220 us
  waiting for transfers between devices  116 us (52%)
  starting transfers between devices  63.3 us (29%)
  Pallas kernels  34.7 us (16%)
  local copies, waits for them, and re-layouts  4.8 us (2%)
    ppermute x33, waiting for transfers between devices, shift(): lax.ppermute(block, axis, [(i, (i + step) % size) for i in range(size)])  79.2 us
    ppermute x33, starting transfers between devices, shift(): lax.ppermute(block, axis, [(i, (i + step) % size) for i in range(size)])  50.3 us
    ppermute x25, waiting for transfers between devices, swap(): return lax.ppermute(block, axis, [(i, i ^ bit) for i in range(size)])  37.1 us
    pallas_call x28, Pallas kernels, call(): pl.pallas_call(body, out_shape=shapes, in_specs=[SM] + [HB if i in hbm el...  31.2 us
    ppermute x25, starting transfers between devices, swap(): return lax.ppermute(block, axis, [(i, i ^ bit) for i in range(size)])  13 us
  transfers between devices with their start and end apart: 58, of which 30 were waited for; matrix products, arithmetic and copies ran while one was open for 0% of the time, Pallas kernels for 12%

commit v1 on v0

--- a/solution.py
+++ b/solution.py
@@ -109,18 +109,24 @@
 def sum_small(small, axis):
     bit = 1
     while bit < lax.axis_size(axis):
-        small = small + swap(small, axis, bit)
+        other = swap(small, axis, bit)
+        small = small + other
         bit *= 2
     return small
 
 
-def swap_dp(message):
+def swap_dp(block):
+    return swap(block, "dp", 1)
+
+
+def sum_rest(keep, recv):
     size = lax.axis_size("dp")
-    bit = 1
-    while bit < size // 2:
-        message = (message.astype(F32) + swap(message, "dp", bit).astype(F32)).astype(BF16)
+    bit = 2
+    while bit < size:
+        keep = (keep.astype(F32) + recv.astype(F32)).astype(BF16)
+        recv = swap(keep, "dp", bit)
         bit *= 2
-    return (message, swap(message, "dp", bit))
+    return (keep, recv)
 
 
 def head_kernel(tokens, vectors, out):
@@ -152,29 +158,32 @@
                 out[:, width:] = w_out[k * height : (k + 1) * height].astype(F32).T.astype(BF16)
 
 
-def ff_pieces_kernel(place, cotangent, w_up, w_down, *refs):
+def ff_pieces_kernel(place, w_up, w_down, *refs):
     outs, sems = refs[:-1], refs[-1]
     cols = len(outs)
     width = w_up.shape[1] // cols
-    high = w_up.shape[0]
-    copies = []
-    for step, out in enumerate(outs):
-        index = target(place, step, cols)
-        pairs = [
-            (w_up.at[:, part(index, width)], out.at[:high]),
-            (w_down.at[part(index, width), :], out.at[high : high + width]),
-            (cotangent, out.at[high + width :]),
+
+    def blocks(of):
+        copies = [
+            pltpu.make_async_copy(of(target(place, step, cols)), out, sems.at[step])
+            for step, out in enumerate(outs)
         ]
-        for i, (there, here) in enumerate(pairs):
-            copies.append(pltpu.make_async_copy(there, here, sems.at[3 * step + i]))
-    for copy in copies:
-        copy.start()
-    for copy in copies:
-        copy.wait()
+        for copy in copies:
+            copy.start()
+        for copy in copies:
+            copy.wait()
+
+    @pl.when(place[2] == 0)
+    def _():
+        blocks(lambda index: w_up.at[:, part(index, width)])
+
+    @pl.when(place[2] == 1)
+    def _():
+        blocks(lambda index: w_down.at[part(index, width), :])
 
 
 def first_norm_kernel(place, *refs):
-    cols = (len(refs) - 5) // 1
+    cols = len(refs) - 5
     pieces, (first_in, normed_out, rstd_out, x_out, vec_out) = refs[:cols], refs[cols:]
     rows = first_in.shape[0]
     feats = pieces[0].shape[1]
@@ -299,23 +308,49 @@
 
 
 def ff_join_kernel(place, *refs):
-    pieces, (up_out, down_out, cot_out) = refs[:-3], refs[-3:]
+    pieces, half_out = refs[:-1], refs[-1]
     cols = len(pieces)
-    feats = pieces[0].shape[1] if cot_out.shape[1] == cols * pieces[0].shape[1] else 0
-    high = up_out.shape[0] // cols
-    width = down_out.shape[0]
+    width = half_out.shape[0] // cols
     for step, piece in enumerate(pieces):
-        at = part(source(place, step, cols), feats)
-        up_out[at, :] = piece[:high]
-        down_out[:, at] = piece[high : high + width]
-        cot_out[:, at] = piece[high + width :]
-
-
-def cot_kernel(place, down, *refs):
+        half_out[part(source(place, step, cols), width), :] = piece[...]
+
+
+def join_lanes_kernel(place, *refs):
+    pieces, out = refs[:-1], refs[-1]
+    feats = pieces[0].shape[1]
+    for step, piece in enumerate(pieces):
+        out[:, part(source(place, step, len(pieces)), feats)] = piece[...]
+
+
+def cat_kernel(place, *refs):
     pieces, out = refs[:-1], refs[-1]
     extent = pieces[0].shape[0]
     for p, piece in enumerate(pieces):
-        out[p * extent : (p + 1) * extent] = mm(piece[...], down[...], 1, 1)
+        out[p * extent : (p + 1) * extent] = piece[...]
+
+
+def cot_kernel(cols, place, mine, other, *refs):
+    pieces, (out, up_out, down_out) = refs[:-3], refs[-3:]
+    extent, width = pieces[0].shape
+
+    @pl.when(place[2] == 0)
+    def _():
+        up_out[...] = mine[...]
+        down_out[...] = other[...]
+
+    @pl.when(place[2] == 1)
+    def _():
+        up_out[...] = other[...]
+        down_out[...] = mine[...]
+
+    feats = width // cols
+    height = down_out.shape[0] // cols
+    for p, piece in enumerate(pieces):
+        total = jnp.zeros((extent, height), F32)
+        for j in range(cols):
+            block = down_out[j * height : (j + 1) * height]
+            total = total + mm(piece[:, j * feats : (j + 1) * feats], block, 1, 1)
+        out[p * extent : (p + 1) * extent] = total
 
 
 def hidden_kernel(place, up, bias, cot_down, *refs):
@@ -342,10 +377,15 @@
     send[...] = mm(grad_out[half:], up[...], 1, 1).astype(BF16)
 
 
-def out_part_kernel(place, act, down, keep, send):
-    half = keep.shape[0]
-    keep[...] = mm(act[:half], down[...], 1, 0)
-    send[...] = mm(act[half:], down[...], 1, 0).astype(BF16)
+def out_part_kernel(cols, place, act, down, keep, send):
+    half, width = keep.shape
+    feats = width // cols
+    height = down.shape[0] // cols
+    for j in range(cols):
+        here = slice(j * feats, (j + 1) * feats)
+        block = down[j * height : (j + 1) * height]
+        keep[:, here] = mm(act[:half], block, 1, 0)
+        send[:, here] = mm(act[half:], block, 1, 0).astype(BF16)
 
 
 def out_features_kernel(place, keep, recv, resid, own, *refs):
@@ -365,11 +405,10 @@
 
 
 def ff_grad_kernel(rows, cols, place, act, grad, bias, *refs):
-    second, cots, out = refs[:rows], refs[rows : 2 * rows], refs[-1]
+    second, cots, (keep, send) = refs[:rows], refs[rows : 2 * rows], refs[2 * rows :]
     extent = second[0].shape[0]
     feats = second[0].shape[1] // cols
     width = grad.shape[1]
-    stride = feats + width
     for j in range(cols):
         here = slice(j * feats, (j + 1) * feats)
         up = jnp.zeros((feats, width), F32)
@@ -378,9 +417,13 @@
             at = slice(p * extent, (p + 1) * extent)
             up = up + mm(second[p][:, here], grad[at], 0, 0)
             down = down + mm(act[at], cots[p][:, here], 0, 0)
-        out[j * stride : j * stride + feats] = up.astype(BF16)
-        out[j * stride + feats : (j + 1) * stride] = down.astype(BF16)
-    out[cols * stride :] = pair_rows(bias[...])
+        there = slice(j * width, (j + 1) * width)
+        even = place[2] == 0
+        keep[there] = jnp.where(even, up, down)
+        send[there] = jnp.where(even, down, up).astype(BF16)
+    ends = pair_rows(bias[...])
+    keep[cols * width :] = ends.astype(F32)
+    send[cols * width :] = ends
 
 
 def pair_rows(vector):
@@ -401,17 +444,32 @@
         out[stride:] = pair_rows(both).astype(out.dtype)
 
 
-def ff_final_kernel(place, *refs):
-    pieces, (up_out, down_out, bias_out) = refs[:-3], refs[-3:]
+def half_join_kernel(place, *refs):
+    pieces, (half_out, bias_out) = refs[:-2], refs[-2:]
     cols = len(pieces)
-    feats = down_out.shape[1]
-    width = up_out.shape[1] // cols
+    width = half_out.shape[0] // cols
     for step, piece in enumerate(pieces):
-        at = part(source(place, step, cols), width)
-        up_out[:, at] = piece[:feats].astype(F32)
-        down_out[at, :] = piece[feats : feats + width].astype(F32)
-        tail = piece[feats + width :].astype(F32)
-        bias_out[:, at] = tail[0:1] + tail[1:2]
+        index = source(place, step, cols)
+        half_out[part(index, width), :] = piece[:width]
+        tail = piece[width:].astype(F32)
+        bias_out[:, part(index, width)] = tail[0:1] + tail[1:2]
+
+
+def ff_final_kernel(place, mine, other, up_out, down_out):
+    def write(up, down):
+        width = up.shape[1]
+        for k in range(up.shape[0] // width):
+            here = slice(k * width, (k + 1) * width)
+            up_out[:, here] = up[here].astype(F32)
+        down_out[...] = down[...].astype(F32)
+
+    @pl.when(place[2] == 0)
+    def _():
+        write(mine, other)
+
+    @pl.when(place[2] == 1)
+    def _():
+        write(other, mine)
 
 
 def second_back_kernel(place, own, *refs):
@@ -437,7 +495,8 @@
 
 def attention_back_kernel(rows, heads, place, wq, wo, q, k, v, ctx, probs, *refs):
     resid = refs[:rows]
-    joined_out, bias_out, keep, send, gctx = refs[rows:]
+    joined_out, keep, send, gctx, bias_out = refs[rows:]
+    size = q.shape[0]
     extent = resid[0].shape[0]
     for p in range(rows):
         at = slice(p * extent, (p + 1) * extent)
@@ -445,7 +504,6 @@
     for h in range(heads):
         here = slice(h * HEAD_DIM, (h + 1) * HEAD_DIM)
         base = 3 * h * HEAD_DIM
-        size = q.shape[0]
         grad_k = jnp.zeros((size, HEAD_DIM), F32)
         grad_v = jnp.zeros((size, HEAD_DIM), F32)
         bias_q = jnp.zeros((1, HEAD_DIM), F32)
@@ -460,32 +518,62 @@
             joined_out[at, base : base + HEAD_DIM] = grad_q.astype(BF16)
             grad_k = grad_k + mm(dscore, q[at, here], 0, 0)
             grad_v = grad_v + mm(prob.astype(BF16), grad, 0, 0)
-        joined_out[:, base + HEAD_DIM : base + 2 * HEAD_DIM] = (grad_k * 0.125).astype(BF16)
-        joined_out[:, base + 2 * HEAD_DIM : base + 3 * HEAD_DIM] = grad_v.astype(BF16)
+        joined_out[:size, base + HEAD_DIM : base + 2 * HEAD_DIM] = (grad_k * 0.125).astype(BF16)
+        joined_out[:size, base + 2 * HEAD_DIM : base + 3 * HEAD_DIM] = grad_v.astype(BF16)
         b = 2 * h * HEAD_DIM
         bias_out[:, b : b + HEAD_DIM] = bias_q
         bias_out[:, b + HEAD_DIM : b + 2 * HEAD_DIM] = jnp.sum(grad_v, 0, keepdims=True)
+    rest = joined_out.shape[1] - bias_out.shape[1]
+    joined_out[size:] = pair_rows(
+        jnp.concatenate([bias_out[...], jnp.zeros((1, rest), F32)], 1)
+    )
     half = keep.shape[0]
     keep[...] = mm(joined_out[:half], wq[...], 1, 1)
-    send[...] = mm(joined_out[half:], wq[...], 1, 1).astype(BF16)
-
-
-def qkv_grad_kernel(rows, place, joined, ctx, bias, *refs):
-    first, resid, out = refs[:rows], refs[rows : 2 * rows], refs[-1]
+    send[...] = mm(joined_out[half:size], wq[...], 1, 1).astype(BF16)
+
+
+def out_grad_kernel(rows, place, ctx, *refs):
+    resid, out = refs[:rows], refs[-1]
+    extent = resid[0].shape[0]
+    total = jnp.zeros(out.shape, F32)
+    for p in range(rows):
+        total = total + mm(ctx[p * extent : (p + 1) * extent], resid[p][...], 0, 0)
+    out[...] = total.astype(BF16)
+
+
+def qkv_own_kernel(rows, place, joined, *refs):
+    first, out = refs[:rows], refs[-1]
     extent = first[0].shape[0]
-    width = joined.shape[1]
-    high = first[0].shape[1]
-    grad = jnp.zeros((high, width), F32)
-    grad_out = jnp.zeros((high, ctx.shape[1]), F32)
+    grad = jnp.zeros(out.shape, F32)
+    for p in range(rows):
+        grad = grad + mm(first[p][...], joined[p * extent : (p + 1) * extent], 0, 0)
+    out[...] = grad
+
+
+def qkv_sum_kernel(rows, bias, place, mine, joined, peer, peer_first, out_a, out_b, *refs):
+    outs, whole = refs[:-1], refs[-1]
+    cols = len(outs)
+    high, width = mine.shape
+    size = joined.shape[0] - PAD
+    extent = size // rows
+    grad = jnp.zeros(mine.shape, F32)
     for p in range(rows):
         at = slice(p * extent, (p + 1) * extent)
-        grad = grad + mm(first[p][...], joined[at], 0, 0)
-        grad_out = grad_out + mm(resid[p][...], ctx[at], 0, 0)
-    out[:high, :width] = grad.astype(BF16)
-    out[:high, width:] = grad_out.astype(BF16)
-    rest = out.shape[1] - bias.shape[1]
-    row = jnp.concatenate([bias[...], jnp.zeros((1, rest), F32)], 1)
-    out[high:] = pair_rows(row)
+        grad = grad + mm(peer_first[at], peer[at], 0, 0)
+    whole[:high, :width] = mine[...] + grad
+    whole[:high, width:] = (out_a[...].astype(F32) + out_b[...].astype(F32)).T
+    ends = joined[size:].astype(F32) + peer[size:].astype(F32)
+    ends = ends[0:1, :bias] + ends[1:2, :bias]
+    ends = jnp.concatenate([ends, jnp.zeros((1, whole.shape[1] - bias), F32)], 1)
+    if cols == 1:
+        outs[0][:high] = whole[...].astype(BF16)
+        outs[0][high:] = pair_rows(ends)
+        return
+    stride = high // cols
+    for step, out in enumerate(outs):
+        at = part(target(place, step, cols), stride)
+        out[:stride] = whole[at, :].astype(out.dtype)
+        out[stride:] = pair_rows(ends).astype(out.dtype)
 
 
 def qkv_final_kernel(place, *refs):
@@ -580,7 +668,8 @@
     rows = lax.axis_size("row")
     own_col = lax.axis_index("col")
     own_row = lax.axis_index("row")
-    place = jnp.stack([own_col, own_row]).astype(jnp.int32)
+    half_id = lax.rem(lax.axis_index("dp"), 2)
+    place = jnp.stack([own_col, own_row, half_id]).astype(jnp.int32)
     extent, feats = tokens.shape
     width = feats * cols
     group = extent * rows
@@ -634,18 +723,15 @@
     )
     first_all = gather_row(first_in)
 
-    cot_late, up_late, down_late = lax.optimization_barrier(
-        (cotangent, w_up, w_down, first_in)
-    )[:3]
+    up_late, down_late = lax.optimization_barrier((w_up, w_down, first_in))[:2]
     ff_blocks = call(
         ff_pieces_kernel,
-        [((feats + ff_cols + extent, feats), BF16)] * cols,
-        place,
-        cot_late,
+        [((ff_cols, feats), BF16)] * cols,
+        place,
         up_late,
         down_late,
-        hbm=(0, 1, 2),
-        scratch=[pltpu.SemaphoreType.DMA((3 * cols,))],
+        hbm=(0, 1),
+        scratch=[pltpu.SemaphoreType.DMA((cols,))],
     )
     ff_in = exchange(ff_blocks)
 
@@ -702,21 +788,26 @@
     )
     second_all = gather_row(second_rows)
 
-    w_up_s, w_down_s, cot_rows = call(
-        ff_join_kernel,
-        [((width, ff_cols), BF16), ((ff_cols, width), BF16), ((extent, width), BF16)],
-        place,
-        *ff_in,
+    (ff_mine,) = call(ff_join_kernel, [((cols * ff_cols, feats), BF16)], place, *ff_in)
+    (cot_rows,) = call(
+        join_lanes_kernel, [((extent, width), BF16)], place, *exchange([cotangent] * cols)
     )
     cot_all = gather_row(cot_rows)
-    (cot_down,) = call(
-        cot_kernel,
-        [((group, ff_cols), F32)],
-        place,
-        w_down_s,
+    cot_down, w_up_s, w_down_s = call(
+        functools.partial(cot_kernel, cols),
+        [
+            ((group, ff_cols), F32),
+            ((cols * ff_cols, feats), BF16),
+            ((cols * ff_cols, feats), BF16),
+        ],
+        place,
+        ff_mine,
+        swap_dp(ff_mine),
         *cot_all,
         flops=2 * group * width * ff_cols,
     )
+    (first_cat,) = call(cat_kernel, [((group, width), BF16)], place, *first_all)
+    peer_first = swap_dp(first_cat)
     (probs,) = call_slopes(
         functools.partial(probs_kernel, order, heads),
         [((heads, group, group), F32)],
@@ -763,7 +854,12 @@
     resid_all = gather_row(resid_rows)
 
     keep, send = call(
-        out_part_kernel, partial_outs, place, act, w_down_s, flops=2 * group * width * ff_cols
+        functools.partial(out_part_kernel, cols),
+        partial_outs,
+        place,
+        act,
+        w_down_s,
+        flops=2 * group * width * ff_cols,
     )
     keep, recv = scatter_row(keep, send, place)
     own, *sends = call(
@@ -784,9 +880,10 @@
         *exchange([own, *sends])[1:],
     )
 
-    (ff_message,) = call(
+    ff_shape = (cols * ff_cols + PAD, feats)
+    ff_keep, ff_send = call(
         functools.partial(ff_grad_kernel, rows, cols),
-        [((cols * (feats + ff_cols) + PAD, ff_cols), BF16)],
+        [(ff_shape, F32), (ff_shape, BF16)],
         place,
         act,
         grad_pre,
@@ -795,23 +892,32 @@
         *cot_all,
         flops=4 * group * width * ff_cols,
     )
-    ff_shape = (feats + ff_cols + PAD, ff_cols)
     ff_sums = call(
         dp_sum_kernel,
-        [(ff_shape, F32)] + [(ff_shape, BF16)] * (cols - 1),
-        place,
-        *swap_dp(ff_message),
-    )
-    grad_w_up, grad_w_down, grad_bias_up = call(
-        ff_final_kernel,
-        [(w_up.shape, F32), (w_down.shape, F32), ((1, bias_up.shape[0]), F32)],
+        [((ff_cols + PAD, feats), BF16)] * cols,
+        place,
+        *sum_rest(ff_keep, swap_dp(ff_send)),
+    )
+    ff_half, grad_bias_up = call(
+        half_join_kernel,
+        [((cols * ff_cols, feats), BF16), ((1, bias_up.shape[0]), F32)],
         place,
         *exchange(ff_sums),
     )
-
-    joined, qv_bias_part, keep, send = call(
+    grad_w_up, grad_w_down = call(
+        ff_final_kernel, [(w_up.shape, F32), (w_down.shape, F32)], place, ff_half, swap_dp(ff_half)
+    )
+
+    (out_mine,) = call(
+        functools.partial(out_grad_kernel, rows),
+        [((out_rows, width), BF16)],
+        place,
+        context,
+        *resid_all,
+    )
+    joined, keep, send = call(
         functools.partial(attention_back_kernel, rows, heads),
-        [((group, qkv_cols), BF16), ((1, 2 * heads * HEAD_DIM), F32)] + partial_outs,
+        [((group + PAD, qkv_cols), BF16)] + partial_outs,
         place,
         wq,
         wo,
@@ -821,26 +927,47 @@
         context,
         probs,
         *resid_all,
-        scratch=[pltpu.VMEM(wide, BF16)],
-    )
-    (qkv_message,) = call(
-        functools.partial(qkv_grad_kernel, rows),
-        [((width + PAD, qkv_cols + out_rows), BF16)],
+        scratch=[pltpu.VMEM(wide, BF16), pltpu.VMEM((1, 2 * heads * HEAD_DIM), F32)],
+    )
+    (qkv_mine,) = call(
+        functools.partial(qkv_own_kernel, rows),
+        [((width, qkv_cols), F32)],
         place,
         joined,
-        context,
-        qv_bias_part,
         *first_all,
-        *resid_all,
-        flops=2 * group * width * (qkv_cols + out_rows),
+        flops=2 * group * width * qkv_cols,
     )
     qkv_shape = (feats + PAD, qkv_cols + out_rows)
+    single = lax.axis_size("dp") == 2
+    whole_shape = (width, qkv_cols + out_rows)
     qkv_sums = call(
-        dp_sum_kernel,
-        [(qkv_shape, F32)] + [(qkv_shape, BF16)] * (cols - 1),
-        place,
-        *swap_dp(qkv_message),
-    )
+        functools.partial(qkv_sum_kernel, rows, 2 * heads * HEAD_DIM),
+        [(qkv_shape, F32)] + [(qkv_shape, BF16)] * (cols - 1)
+        if single
+        else [((width + PAD, qkv_cols + out_rows), BF16)],
+        place,
+        qkv_mine,
+        joined,
+        swap_dp(joined),
+        peer_first,
+        out_mine,
+        swap_dp(out_mine),
+        scratch=[pltpu.VMEM(whole_shape, F32)],
+        flops=2 * group * width * qkv_cols,
+    )
+    if not single:
+        message = qkv_sums[0]
+        bit = 2
+        while bit < lax.axis_size("dp") // 2:
+            message = (message.astype(F32) + swap(message, "dp", bit).astype(F32)).astype(BF16)
+            bit *= 2
+        qkv_sums = call(
+            dp_sum_kernel,
+            [(qkv_shape, F32)] + [(qkv_shape, BF16)] * (cols - 1),
+            place,
+            message,
+            swap(message, "dp", bit),
+        )
     grad_w_qkv, grad_w_out, grad_bias_qv = call(
         qkv_final_kernel,
         [(w_qkv.shape, F32), (w_out.shape, F32), ((1, bias_qv.shape[0]), F32)],

time: 221 us -> 236 us (1.068)
  starting transfers between devices: 63.3 us -> 78.3 us
  Pallas kernels: 34.7 us -> 37.1 us
    ppermute x33 -> x36, waiting for transfers between devices: 79.2 us -> 47.2 us  [shift(): lax.ppermute(block, axis, [(i, (i + step) % size) for i in range(size)])]
    ppermute x25 -> x29, waiting for transfers between devices: 37.1 us -> 66.9 us  [swap(): return lax.ppermute(block, axis, [(i, i ^ bit) for i in range(size)])]
    ppermute x33 -> x36, starting transfers between devices: 50.3 us -> 61.4 us  [shift(): lax.ppermute(block, axis, [(i, (i + step) % size) for i in range(size)])]
    ppermute x25 -> x29, starting transfers between devices: 13 us -> 16.8 us  [swap(): return lax.ppermute(block, axis, [(i, i ^ bit) for i in range(size)])]
    pallas_call x28 -> x32, Pallas kernels: 31.2 us -> 33.6 us  [call(): pl.pallas_call(body, out_shape=shapes, in_specs=[SM] + [HB if i in hbm el...]
  transfers between devices with their start and end apart: 58 -> 65, of which waited for: 30 -> 27; matrix products, arithmetic and copies ran while one was open for 0% -> 0% of each run, Pallas kernels for 12% -> 12%
where the time goes in v1:
time: 236 us; the launch traced here: 235 us
  waiting for transfers between devices  114 us (48%)
  starting transfers between devices  78.3 us (33%)
  Pallas kernels  37.1 us (16%)
  local copies, waits for them, and re-layouts  4.8 us (2%)
    ppermute x29, waiting for transfers between devices, swap(): return lax.ppermute(block, axis, [(i, i ^ bit) for i in range(size)])  66.9 us
    ppermute x36, starting transfers between devices, shift(): lax.ppermute(block, axis, [(i, (i + step) % size) for i in range(size)])  61.4 us
    ppermute x36, waiting for transfers between devices, shift(): lax.ppermute(block, axis, [(i, (i + step) % size) for i in range(size)])  47.2 us
    pallas_call x32, Pallas kernels, call(): pl.pallas_call(body, out_shape=shapes, in_specs=[SM] + [HB if i in hbm el...  33.6 us
    ppermute x29, starting transfers between devices, swap(): return lax.ppermute(block, axis, [(i, i ^ bit) for i in range(size)])  16.8 us
  transfers between devices with their start and end apart: 65, of which 27 were waited for; matrix products, arithmetic and copies ran while one was open for 0% of the time, Pallas kernels for 12%

profile of v1, /device:TPU:0, one launch (start us, length us, event | category | flops | bytes accessed | tf_op | source)
XLA Modules:
  0.0 235.4 jit_solution(8387304998082067285)
XLA Ops:
  2.3 3.1 %collective-permute-start = (bf16[144,256]{1,0:T(8,128)(2,1)S(1)}, bf16[144,256]{1,0:T(8,128)(2,1)S(1)}, u32[]{:S(2)}, u32[]{:S(2)}) collective-permute-start(bf16[144,256]{1,0:T(8,128)(2,1)S(1)} %head.1.refs_0_), channel_id=1, source_target_pairs={{0,1},{1,2},{2,3},{3,0},{4,5},{5,6},{6,7},{7,4},{8,9},{9,10},{10,1... | collective-permute-start | bytes 221192 | tf_op jit(solution)/shard_map/ppermute | solution.py:87
  5.4 2.6 %collective-permute-start.1 = (bf16[144,256]{1,0:T(8,128)(2,1)S(1)}, bf16[144,256]{1,0:T(8,128)(2,1)S(1)}, u32[]{:S(2)}, u32[]{:S(2)}) collective-permute-start(bf16[144,256]{1,0:T(8,128)(2,1)S(1)} %head.1.refs_0_), channel_id=1, source_target_pairs={{0,2},{1,3},{2,0},{3,1},{4,6},{5,7},{6,4},{7,5},{8,10},{9,11},{10,... | collective-permute-start | bytes 221192 | tf_op jit(solution)/shard_map/ppermute | solution.py:87
  8.0 1.3 collective-permute-start.2
  10.1 2.9 %collective-permute-done.1.refs_2_ = bf16[144,256]{1,0:T(8,128)(2,1)S(1)} collective-permute-done((bf16[144,256]{1,0:T(8,128)(2,1)S(1)}, bf16[144,256]{1,0:T(8,128)(2,1)S(1)}, u32[]{:S(2)}, u32[]{:S(2)}) %collective-permute-start.1) | collective-permute-done | bytes 73760 | tf_op jit(solution)/shard_map/ppermute | solution.py:87
  14.0 1.6 collective-permute-start.13
  15.5 6.4 %collective-permute-done.13.refs_2_.refs_1_ = bf16[128,1024]{1,0:T(8,128)(2,1)S(1)} collective-permute-done((bf16[128,1024]{1,0:T(8,128)(2,1)S(1)}, bf16[128,1024]{1,0:T(8,128)(2,1)S(1)}, u32[]{:S(2)}, u32[]{:S(2)}) %collective-permute-start.13) | collective-permute-done | bytes 262176 | tf_op jit(solution)/shard_map/ppermute | solution.py:92
  23.8 1.8 shard_map.250
  25.7 2.2 collective-permute-start.16
  29.0 1.3 collective-permute-start.18
  30.4 3.7 %collective-permute-done.16.refs_6_ = bf16[256,256]{1,0:T(8,128)(2,1)S(1)} collective-permute-done((bf16[256,256]{1,0:T(8,128)(2,1)S(1)}, bf16[256,256]{1,0:T(8,128)(2,1)S(1)}, u32[]{:S(2)}, u32[]{:S(2)}) %collective-permute-start.16) | collective-permute-done | bytes 131104 | tf_op jit(solution)/shard_map/ppermute | solution.py:87
  34.0 5.1 %collective-permute-done.17.refs_7_ = bf16[256,256]{1,0:T(8,128)(2,1)S(1)} collective-permute-done((bf16[256,256]{1,0:T(8,128)(2,1)S(1)}, bf16[256,256]{1,0:T(8,128)(2,1)S(1)}, u32[]{:S(2)}, u32[]{:S(2)}) %collective-permute-start.17) | collective-permute-done | bytes 131104 | tf_op jit(solution)/shard_map/ppermute | solution.py:87
  39.8 2.3 shard_map.251
  42.2 1.9 collective-permute-done.19.recv
  44.8 1.3 collective-permute-start.20
  46.1 3.3 %collective-permute-start.7 = (bf16[128,256]{1,0:T(8,128)(2,1)S(1)}, bf16[128,256]{1,0:T(8,128)(2,1)S(1)}, u32[]{:S(2)}, u32[]{:S(2)}) collective-permute-start(bf16[128,256]{1,0:T(8,128)(2,1)S(1)} %copy-done.4), channel_id=1, source_target_pairs={{0,1},{1,2},{2,3},{3,0},{4,5},{5,6},{6,7},{7,4},{8,9},{9,10},{10,1... | collective-permute-start | bytes 196616 | tf_op jit(solution)/shard_map/ppermute | solution.py:87
  49.4 3.8 %collective-permute-done.20.recv = bf16[128,1024]{1,0:T(8,128)(2,1)S(1)} collective-permute-done((bf16[128,1024]{1,0:T(8,128)(2,1)S(1)}, bf16[128,1024]{1,0:T(8,128)(2,1)S(1)}, u32[]{:S(2)}, u32[]{:S(2)}) %collective-permute-start.20) | collective-permute-done | bytes 262176 | tf_op jit(solution)/shard_map/ppermute | solution.py:92
  53.8 3.3 %collective-permute-start.21 = (bf16[32,1024]{1,0:T(8,128)(2,1)S(1)}, bf16[32,1024]{1,0:T(8,128)(2,1)S(1)}, u32[]{:S(2)}, u32[]{:S(2)}) collective-permute-start(bf16[32,1024]{1,0:T(8,128)(2,1)S(1)} %get-tuple-element.119), channel_id=1, source_target_pairs={{0,1},{1,2},{2,3},{3,0},{4,5},{5,6},{6,7},{7,4},{8,9},{9,10},{10,1... | collective-permute-start | bytes 196616 | tf_op jit(solution)/shard_map/ppermute | solution.py:87
  58.1 1.5 collective-permute-start.23
  60.9 2.0 collective-permute-start.4
  62.8 1.4 collective-permute-start.5
  64.2 2.0 collective-permute-start.8
  67.9 10.9 %collective-permute-done.8.refs_2_ = bf16[128,256]{1,0:T(8,128)(2,1)S(1)} collective-permute-done((bf16[128,256]{1,0:T(8,128)(2,1)S(1)}, bf16[128,256]{1,0:T(8,128)(2,1)S(1)}, u32[]{:S(2)}, u32[]{:S(2)}) %collective-permute-start.8) | collective-permute-done | bytes 65568 | tf_op jit(solution)/shard_map/ppermute | solution.py:87
  78.9 2.4 %collective-permute-start.25 = (bf16[32,1024]{1,0:T(8,128)(2,1)S(1)}, bf16[32,1024]{1,0:T(8,128)(2,1)S(1)}, u32[]{:S(2)}, u32[]{:S(2)}) collective-permute-start(bf16[32,1024]{1,0:T(8,128)(2,1)S(1)} %get-tuple-element.124.refs_0_), channel_id=1, source_target_pairs={{0,2},{1,3},{2,0},{3,1},{4,6},{5,7},{6,4},{7,5},{8,10},{9,11},{10,... | collective-permute-start | bytes 196616 | tf_op jit(solution)/shard_map/ppermute | solution.py:87
  81.3 1.5 collective-permute-start.26
  83.4 1.3 collective-permute-start.10
  85.3 1.6 collective-permute-start.6
  88.2 2.7 %collective-permute-done.10.refs_1_.refs_5_ = bf16[128,1024]{1,0:T(8,128)(2,1)S(1)} collective-permute-done((bf16[128,1024]{1,0:T(8,128)(2,1)S(1)}, bf16[128,1024]{1,0:T(8,128)(2,1)S(1)}, u32[]{:S(2)}, u32[]{:S(2)}) %collective-permute-start.10) | collective-permute-done | bytes 262176 | tf_op jit(solution)/shard_map/ppermute | solution.py:92
  91.5 4.1 %collective-permute-done.27.refs_1_ = bf16[128,1024]{1,0:T(8,128)(2,1)S(1)} collective-permute-done((bf16[128,1024]{1,0:T(8,128)(2,1)S(1)}, bf16[128,1024]{1,0:T(8,128)(2,1)S(1)}, u32[]{:S(2)}, u32[]{:S(2)}) %collective-permute-start.27) | collective-permute-done | bytes 262176 | tf_op jit(solution)/shard_map/ppermute | solution.py:92
  95.5 1.6 collective-permute-done.6.other
  97.1 1.4 shard_map.249
  98.6 1.6 shard_map.256
  100.3 1.9 collective-permute-done.35.recv
  103.7 7.5 %collective-permute-done.36.recv = bf16[128,1024]{1,0:T(8,128)(2,1)S(1)} collective-permute-done((bf16[128,1024]{1,0:T(8,128)(2,1)S(1)}, bf16[128,1024]{1,0:T(8,128)(2,1)S(1)}, u32[]{:S(2)}, u32[]{:S(2)}) %collective-permute-start.36) | collective-permute-done | bytes 262176 | tf_op jit(solution)/shard_map/ppermute | solution.py:92
  113.4 2.7 %collective-permute-start.39 = (bf16[32,1024]{1,0:T(8,128)(2,1)S(1)}, bf16[32,1024]{1,0:T(8,128)(2,1)S(1)}, u32[]{:S(2)}, u32[]{:S(2)}) collective-permute-start(bf16[32,1024]{1,0:T(8,128)(2,1)S(1)} %get-tuple-element.152), channel_id=1, source_target_pairs={{0,3},{1,0},{2,1},{3,2},{4,7},{5,4},{6,5},{7,6},{8,11},{9,8},{10,9... | collective-permute-start | bytes 196616 | tf_op jit(solution)/shard_map/ppermute | solution.py:87
  116.1 2.4 %collective-permute-done.37.refs_0_ = bf16[32,1024]{1,0:T(8,128)(2,1)S(1)} collective-permute-done((bf16[32,1024]{1,0:T(8,128)(2,1)S(1)}, bf16[32,1024]{1,0:T(8,128)(2,1)S(1)}, u32[]{:S(2)}, u32[]{:S(2)}) %collective-permute-start.37) | collective-permute-done | bytes 65568 | tf_op jit(solution)/shard_map/ppermute | solution.py:87
  118.5 1.7 collective-permute-done.38.refs_1_
  120.9 1.6 collective-permute-start.40
  123.7 1.3 collective-permute-start.42
  125.0 2.5 %collective-permute-done.40.refs_1_ = bf16[32,1024]{1,0:T(8,128)(2,1)S(1)} collective-permute-done((bf16[32,1024]{1,0:T(8,128)(2,1)S(1)}, bf16[32,1024]{1,0:T(8,128)(2,1)S(1)}, u32[]{:S(2)}, u32[]{:S(2)}) %collective-permute-start.40) | collective-permute-done | bytes 65568 | tf_op jit(solution)/shard_map/ppermute | solution.py:87
  127.5 1.8 collective-permute-done.41.refs_2_
  130.8 6.0 %collective-permute-done.43.refs_1_ = bf16[128,1024]{1,0:T(8,128)(2,1)S(1)} collective-permute-done((bf16[128,1024]{1,0:T(8,128)(2,1)S(1)}, bf16[128,1024]{1,0:T(8,128)(2,1)S(1)}, u32[]{:S(2)}, u32[]{:S(2)}) %collective-permute-start.43) | collective-permute-done | bytes 262176 | tf_op jit(solution)/shard_map/ppermute | solution.py:92
  138.2 1.8 shard_map.275
  140.1 1.3 collective-permute-start.60
  142.6 2.5 %shard_map.266 = (bf16[528,192]{1,0:T(8,128)(2,1)S(1)}, f32[256,1024]{1,0:T(8,128)S(1)}, bf16[256,1024]{1,0:T(8,128)(2,1)S(1)}) custom-call(s32[3]{0:T(128)S(1)} %pad_add_fusion.place.place_ref, bf16[1024,192]{1,0:T(8,128)(2,1)S(1)} %get-tuple-element.138.wq, bf16[1024,64]{1,0:T(8,128)(2,1)S(1)} %get-tuple-element.139.wo, ...), custom_call_target="tpu_custom_call" | custom-call | bytes 4659200 | tf_op jit(solution)/shard_map/pallas_call | solution.py:33
  146.7 27.7 %collective-permute-done.60.other = bf16[1040,256]{1,0:T(8,128)(2,1)S(1)} collective-permute-done((bf16[1040,256]{1,0:T(8,128)(2,1)S(1)}, bf16[1040,256]{1,0:T(8,128)(2,1)S(1)}, u32[]{:S(2)}, u32[]{:S(2)}) %collective-permute-start.60) | collective-permute-done | bytes 532512 | tf_op jit(solution)/shard_map/ppermute | solution.py:92
  175.1 2.6 %collective-permute-start.61 = (bf16[272,256]{1,0:T(8,128)(2,1)S(1)}, bf16[272,256]{1,0:T(8,128)(2,1)S(1)}, u32[]{:S(2)}, u32[]{:S(2)}) collective-permute-start(bf16[272,256]{1,0:T(8,128)(2,1)S(1)} %get-tuple-element.181), channel_id=1, source_target_pairs={{0,1},{1,2},{2,3},{3,0},{4,5},{5,6},{6,7},{7,4},{8,9},{9,10},{10,1... | collective-permute-start | bytes 417800 | tf_op jit(solution)/shard_map/ppermute | solution.py:87
  177.6 2.4 %collective-permute-start.63 = (bf16[272,256]{1,0:T(8,128)(2,1)S(1)}, bf16[272,256]{1,0:T(8,128)(2,1)S(1)}, u32[]{:S(2)}, u32[]{:S(2)}) collective-permute-start(bf16[272,256]{1,0:T(8,128)(2,1)S(1)} %get-tuple-element.183), channel_id=1, source_target_pairs={{0,3},{1,0},{2,1},{3,2},{4,7},{5,4},{6,5},{7,6},{8,11},{9,8},{10,9... | collective-permute-start | bytes 417800 | tf_op jit(solution)/shard_map/ppermute | solution.py:87
  182.0 1.6 collective-permute-done.61.refs_1_
  184.0 4.2 %collective-permute-done.62.refs_2_ = bf16[272,256]{1,0:T(8,128)(2,1)S(1)} collective-permute-done((bf16[272,256]{1,0:T(8,128)(2,1)S(1)}, bf16[272,256]{1,0:T(8,128)(2,1)S(1)}, u32[]{:S(2)}, u32[]{:S(2)}) %collective-permute-start.62) | collective-permute-done | bytes 139296 | tf_op jit(solution)/shard_map/ppermute | solution.py:87
  191.1 3.5 %collective-permute-start.48 = (bf16[144,256]{1,0:T(8,128)(2,1)S(1)}, bf16[144,256]{1,0:T(8,128)(2,1)S(1)}, u32[]{:S(2)}, u32[]{:S(2)}) collective-permute-start(bf16[144,256]{1,0:T(8,128)(2,1)S(1)} %get-tuple-element.163), channel_id=1, source_target_pairs={{0,1},{1,2},{2,3},{3,0},{4,5},{5,6},{6,7},{7,4},{8,9},{9,10},{10,1... | collective-permute-start | bytes 221192 | tf_op jit(solution)/shard_map/ppermute | solution.py:87
  195.8 1.4 collective-permute-start.49
  198.9 2.5 %collective-permute-done.49.refs_1_ = bf16[144,256]{1,0:T(8,128)(2,1)S(1)} collective-permute-done((bf16[144,256]{1,0:T(8,128)(2,1)S(1)}, bf16[144,256]{1,0:T(8,128)(2,1)S(1)}, u32[]{:S(2)}, u32[]{:S(2)}) %collective-permute-start.49) | collective-permute-done | bytes 73760 | tf_op jit(solution)/shard_map/ppermute | solution.py:87
  202.6 3.2 %collective-permute-done.50.refs_2_ = bf16[144,256]{1,0:T(8,128)(2,1)S(1)} collective-permute-done((bf16[144,256]{1,0:T(8,128)(2,1)S(1)}, bf16[144,256]{1,0:T(8,128)(2,1)S(1)}, u32[]{:S(2)}, u32[]{:S(2)}) %collective-permute-start.50) | collective-permute-done | bytes 73760 | tf_op jit(solution)/shard_map/ppermute | solution.py:87
  205.8 1.3 shard_map.270.mine
  207.1 1.4 shard_map.269
  208.5 3.2 %collective-permute-start.33 = (bf16[128,256]{1,0:T(8,128)(2,1)S(1)}, bf16[128,256]{1,0:T(8,128)(2,1)S(1)}, u32[]{:S(2)}, u32[]{:S(2)}) collective-permute-start(bf16[128,256]{1,0:T(8,128)(2,1)S(1)} %get-tuple-element.134), channel_id=1, source_target_pairs={{0,2},{1,3},{2,0},{3,1},{4,6},{5,7},{6,4},{7,5},{8,10},{9,11},{10,... | collective-permute-start | bytes 196616 | tf_op jit(solution)/shard_map/ppermute | solution.py:87
  211.7 1.5 shard_map.273
  213.2 3.6 %collective-permute-start.57 = (bf16[272,256]{1,0:T(8,128)(2,1)S(1)}, bf16[272,256]{1,0:T(8,128)(2,1)S(1)}, u32[]{:S(2)}, u32[]{:S(2)}) collective-permute-start(bf16[272,256]{1,0:T(8,128)(2,1)S(1)} %get-tuple-element.170), channel_id=1, source_target_pairs={{0,1},{1,2},{2,3},{3,0},{4,5},{5,6},{6,7},{7,4},{8,9},{9,10},{10,1... | collective-permute-start | bytes 417800 | tf_op jit(solution)/shard_map/ppermute | solution.py:87
  217.2 2.0 collective-permute-start.59
  219.7 3.3 %collective-permute-done.52 = f32[8,256]{1,0:T(8,128)S(1)} collective-permute-done((f32[8,256]{1,0:T(8,128)S(1)}, f32[8,256]{1,0:T(8,128)S(1)}, u32[]{:S(2)}, u32[]{:S(2)}) %collective-permute-start.52) | collective-permute-done | bytes 8224 | tf_op jit(solution)/shard_map/ppermute | solution.py:92
  222.9 1.9 collective-permute-start.34
  224.9 3.6 %collective-permute-done.34.refs_2_ = bf16[128,256]{1,0:T(8,128)(2,1)S(1)} collective-permute-done((bf16[128,256]{1,0:T(8,128)(2,1)S(1)}, bf16[128,256]{1,0:T(8,128)(2,1)S(1)}, u32[]{:S(2)}, u32[]{:S(2)}) %collective-permute-start.34) | collective-permute-done | bytes 65568 | tf_op jit(solution)/shard_map/ppermute | solution.py:87
  230.6 2.0 shard_map.278
  232.6 2.2 shard_map.274
  (127 shorter events, 40.4 us)
Async XLA Ops:
  2.3 7.8 %collective-permute-start = (bf16[144,256]{1,0:T(8,128)(2,1)S(1)}, bf16[144,256]{1,0:T(8,128)(2,1)S(1)}, u32[]{:S(2)}, u32[]{:S(2)}) collective-permute-start(bf16[144,256]{1,0:T(8,128)(2,1)S(1)} %head.1.refs_0_), channel_id=1, source_target_pairs={{0,1},{1,2},{2,3},{3,0},{4,5},{5,6},{6,7},{7,4},{8,9},{9,10},{10,1... | collective-permute-start | bytes 221192 | tf_op jit(solution)/shard_map/ppermute | solution.py:87
  5.4 7.5 %collective-permute-start.1 = (bf16[144,256]{1,0:T(8,128)(2,1)S(1)}, bf16[144,256]{1,0:T(8,128)(2,1)S(1)}, u32[]{:S(2)}, u32[]{:S(2)}) collective-permute-start(bf16[144,256]{1,0:T(8,128)(2,1)S(1)} %head.1.refs_0_), channel_id=1, source_target_pairs={{0,2},{1,3},{2,0},{3,1},{4,6},{5,7},{6,4},{7,5},{8,10},{9,11},{10,... | collective-permute-start | bytes 221192 | tf_op jit(solution)/shard_map/ppermute | solution.py:87
  8.0 5.2 %collective-permute-start.2 = (bf16[144,256]{1,0:T(8,128)(2,1)S(1)}, bf16[144,256]{1,0:T(8,128)(2,1)S(1)}, u32[]{:S(2)}, u32[]{:S(2)}) collective-permute-start(bf16[144,256]{1,0:T(8,128)(2,1)S(1)} %head.1.refs_0_), channel_id=1, source_target_pairs={{0,3},{1,0},{2,1},{3,2},{4,7},{5,4},{6,5},{7,6},{8,11},{9,8},{10,9... | collective-permute-start | bytes 221192 | tf_op jit(solution)/shard_map/ppermute | solution.py:87
  14.0 8.0 %collective-permute-start.13 = (bf16[128,1024]{1,0:T(8,128)(2,1)S(1)}, bf16[128,1024]{1,0:T(8,128)(2,1)S(1)}, u32[]{:S(2)}, u32[]{:S(2)}) collective-permute-start(bf16[128,1024]{1,0:T(8,128)(2,1)S(1)} %get-tuple-element.101.refs_1_.refs_0_), channel_id=1, source_target_pairs={{0,8},{4,12},{8,0},{12,4},{1,9},{5,13},{9,1},{13,5},{2,10},{6,14},... | collective-permute-start | bytes 786440 | tf_op jit(solution)/shard_map/ppermute | solution.py:92
  15.5 23.6 %collective-permute-start.14 = (bf16[128,1024]{1,0:T(8,128)(2,1)S(1)}, bf16[128,1024]{1,0:T(8,128)(2,1)S(1)}, u32[]{:S(2)}, u32[]{:S(2)}) collective-permute-start(bf16[128,1024]{1,0:T(8,128)(2,1)S(1)} %get-tuple-element.101.refs_1_.refs_0_), channel_id=1, source_target_pairs={{0,4},{4,0},{8,12},{12,8},{1,5},{5,1},{9,13},{13,9},{2,6},{6,2},{1... | collective-permute-start | bytes 786440 | tf_op jit(solution)/shard_map/ppermute | solution.py:92
  21.9 17.2 %collective-permute-start.15 = (bf16[128,1024]{1,0:T(8,128)(2,1)S(1)}, bf16[128,1024]{1,0:T(8,128)(2,1)S(1)}, u32[]{:S(2)}, u32[]{:S(2)}) collective-permute-start(bf16[128,1024]{1,0:T(8,128)(2,1)S(1)} %collective-permute-done.13.refs_2_.refs_1_), channel_id=1, source_target_pairs={{0,4},{4,0},{8,12},{12,8},{1,5},{5,1},{9,13},{13,9},{2,6},{6,2},{1... | collective-permute-start | bytes 786440 | tf_op jit(solution)/shard_map/ppermute | solution.py:92
  25.7 8.3 %collective-permute-start.16 = (bf16[256,256]{1,0:T(8,128)(2,1)S(1)}, bf16[256,256]{1,0:T(8,128)(2,1)S(1)}, u32[]{:S(2)}, u32[]{:S(2)}) collective-permute-start(bf16[256,256]{1,0:T(8,128)(2,1)S(1)} %get-tuple-element.111), channel_id=1, source_target_pairs={{0,1},{1,2},{2,3},{3,0},{4,5},{5,6},{6,7},{7,4},{8,9},{9,10},{10,1... | collective-permute-start | bytes 393224 | tf_op jit(solution)/shard_map/ppermute | solution.py:87
  27.9 11.3 %collective-permute-start.17 = (bf16[256,256]{1,0:T(8,128)(2,1)S(1)}, bf16[256,256]{1,0:T(8,128)(2,1)S(1)}, u32[]{:S(2)}, u32[]{:S(2)}) collective-permute-start(bf16[256,256]{1,0:T(8,128)(2,1)S(1)} %get-tuple-element.112), channel_id=1, source_target_pairs={{0,2},{1,3},{2,0},{3,1},{4,6},{5,7},{6,4},{7,5},{8,10},{9,11},{10,... | collective-permute-start | bytes 393224 | tf_op jit(solution)/shard_map/ppermute | solution.py:87
  29.0 10.1 %collective-permute-start.18 = (bf16[256,256]{1,0:T(8,128)(2,1)S(1)}, bf16[256,256]{1,0:T(8,128)(2,1)S(1)}, u32[]{:S(2)}, u32[]{:S(2)}) collective-permute-start(bf16[256,256]{1,0:T(8,128)(2,1)S(1)} %get-tuple-element.113), channel_id=1, source_target_pairs={{0,3},{1,0},{2,1},{3,2},{4,7},{5,4},{6,5},{7,6},{8,11},{9,8},{10,9... | collective-permute-start | bytes 393224 | tf_op jit(solution)/shard_map/ppermute | solution.py:87
  42.1 2.0 collective-permute-start.19
  44.8 8.4 %collective-permute-start.20 = (bf16[128,1024]{1,0:T(8,128)(2,1)S(1)}, bf16[128,1024]{1,0:T(8,128)(2,1)S(1)}, u32[]{:S(2)}, u32[]{:S(2)}) collective-permute-start(bf16[128,1024]{1,0:T(8,128)(2,1)S(1)} %get-tuple-element.117), channel_id=1, source_target_pairs={{0,8},{4,12},{8,0},{12,4},{1,9},{5,13},{9,1},{13,5},{2,10},{6,14},... | collective-permute-start | bytes 786440 | tf_op jit(solution)/shard_map/ppermute | solution.py:92
  46.1 14.7 %collective-permute-start.7 = (bf16[128,256]{1,0:T(8,128)(2,1)S(1)}, bf16[128,256]{1,0:T(8,128)(2,1)S(1)}, u32[]{:S(2)}, u32[]{:S(2)}) collective-permute-start(bf16[128,256]{1,0:T(8,128)(2,1)S(1)} %copy-done.4), channel_id=1, source_target_pairs={{0,1},{1,2},{2,3},{3,0},{4,5},{5,6},{6,7},{7,4},{8,9},{9,10},{10,1... | collective-permute-start | bytes 196616 | tf_op jit(solution)/shard_map/ppermute | solution.py:87
  53.8 9.0 %collective-permute-start.21 = (bf16[32,1024]{1,0:T(8,128)(2,1)S(1)}, bf16[32,1024]{1,0:T(8,128)(2,1)S(1)}, u32[]{:S(2)}, u32[]{:S(2)}) collective-permute-start(bf16[32,1024]{1,0:T(8,128)(2,1)S(1)} %get-tuple-element.119), channel_id=1, source_target_pairs={{0,1},{1,2},{2,3},{3,0},{4,5},{5,6},{6,7},{7,4},{8,9},{9,10},{10,1... | collective-permute-start | bytes 196616 | tf_op jit(solution)/shard_map/ppermute | solution.py:87
  57.1 7.1 %collective-permute-start.22 = (bf16[32,1024]{1,0:T(8,128)(2,1)S(1)}, bf16[32,1024]{1,0:T(8,128)(2,1)S(1)}, u32[]{:S(2)}, u32[]{:S(2)}) collective-permute-start(bf16[32,1024]{1,0:T(8,128)(2,1)S(1)} %get-tuple-element.120), channel_id=1, source_target_pairs={{0,2},{1,3},{2,0},{3,1},{4,6},{5,7},{6,4},{7,5},{8,10},{9,11},{10,... | collective-permute-start | bytes 196616 | tf_op jit(solution)/shard_map/ppermute | solution.py:87
  58.1 8.1 %collective-permute-start.23 = (bf16[32,1024]{1,0:T(8,128)(2,1)S(1)}, bf16[32,1024]{1,0:T(8,128)(2,1)S(1)}, u32[]{:S(2)}, u32[]{:S(2)}) collective-permute-start(bf16[32,1024]{1,0:T(8,128)(2,1)S(1)} %get-tuple-element.121), channel_id=1, source_target_pairs={{0,3},{1,0},{2,1},{3,2},{4,7},{5,4},{6,5},{7,6},{8,11},{9,8},{10,9... | collective-permute-start | bytes 196616 | tf_op jit(solution)/shard_map/ppermute | solution.py:87
  60.3 21.0 %collective-permute-start.3 = (bf16[256,256]{1,0:T(8,128)(2,1)S(1)}, bf16[256,256]{1,0:T(8,128)(2,1)S(1)}, u32[]{:S(2)}, u32[]{:S(2)}) collective-permute-start(bf16[256,256]{1,0:T(8,128)(2,1)S(1)} %get-tuple-element.105), channel_id=1, source_target_pairs={{0,1},{1,2},{2,3},{3,0},{4,5},{5,6},{6,7},{7,4},{8,9},{9,10},{10,1... | collective-permute-start | bytes 393224 | tf_op jit(solution)/shard_map/ppermute | solution.py:87
  60.9 22.5 %collective-permute-start.4 = (bf16[256,256]{1,0:T(8,128)(2,1)S(1)}, bf16[256,256]{1,0:T(8,128)(2,1)S(1)}, u32[]{:S(2)}, u32[]{:S(2)}) collective-permute-start(bf16[256,256]{1,0:T(8,128)(2,1)S(1)} %get-tuple-element.106), channel_id=1, source_target_pairs={{0,2},{1,3},{2,0},{3,1},{4,6},{5,7},{6,4},{7,5},{8,10},{9,11},{10,... | collective-permute-start | bytes 393224 | tf_op jit(solution)/shard_map/ppermute | solution.py:87
  62.8 21.9 %collective-permute-start.5 = (bf16[256,256]{1,0:T(8,128)(2,1)S(1)}, bf16[256,256]{1,0:T(8,128)(2,1)S(1)}, u32[]{:S(2)}, u32[]{:S(2)}) collective-permute-start(bf16[256,256]{1,0:T(8,128)(2,1)S(1)} %get-tuple-element.107), channel_id=1, source_target_pairs={{0,3},{1,0},{2,1},{3,2},{4,7},{5,4},{6,5},{7,6},{8,11},{9,8},{10,9... | collective-permute-start | bytes 393224 | tf_op jit(solution)/shard_map/ppermute | solution.py:87
  64.2 14.7 %collective-permute-start.8 = (bf16[128,256]{1,0:T(8,128)(2,1)S(1)}, bf16[128,256]{1,0:T(8,128)(2,1)S(1)}, u32[]{:S(2)}, u32[]{:S(2)}) collective-permute-start(bf16[128,256]{1,0:T(8,128)(2,1)S(1)} %copy-done.4), channel_id=1, source_target_pairs={{0,2},{1,3},{2,0},{3,1},{4,6},{5,7},{6,4},{7,5},{8,10},{9,11},{10,... | collective-permute-start | bytes 196616 | tf_op jit(solution)/shard_map/ppermute | solution.py:87
  66.2 12.7 %collective-permute-start.9 = (bf16[128,256]{1,0:T(8,128)(2,1)S(1)}, bf16[128,256]{1,0:T(8,128)(2,1)S(1)}, u32[]{:S(2)}, u32[]{:S(2)}) collective-permute-start(bf16[128,256]{1,0:T(8,128)(2,1)S(1)} %copy-done.4), channel_id=1, source_target_pairs={{0,3},{1,0},{2,1},{3,2},{4,7},{5,4},{6,5},{7,6},{8,11},{9,8},{10,9... | collective-permute-start | bytes 196616 | tf_op jit(solution)/shard_map/ppermute | solution.py:87
  78.9 8.0 %collective-permute-start.24 = (bf16[32,1024]{1,0:T(8,128)(2,1)S(1)}, bf16[32,1024]{1,0:T(8,128)(2,1)S(1)}, u32[]{:S(2)}, u32[]{:S(2)}) collective-permute-start(bf16[32,1024]{1,0:T(8,128)(2,1)S(1)} %get-tuple-element.124.refs_0_), channel_id=1, source_target_pairs={{0,1},{1,2},{2,3},{3,0},{4,5},{5,6},{6,7},{7,4},{8,9},{9,10},{10,1... | collective-permute-start | bytes 196616 | tf_op jit(solution)/shard_map/ppermute | solution.py:87
  78.9 8.0 %collective-permute-start.25 = (bf16[32,1024]{1,0:T(8,128)(2,1)S(1)}, bf16[32,1024]{1,0:T(8,128)(2,1)S(1)}, u32[]{:S(2)}, u32[]{:S(2)}) collective-permute-start(bf16[32,1024]{1,0:T(8,128)(2,1)S(1)} %get-tuple-element.124.refs_0_), channel_id=1, source_target_pairs={{0,2},{1,3},{2,0},{3,1},{4,6},{5,7},{6,4},{7,5},{8,10},{9,11},{10,... | collective-permute-start | bytes 196616 | tf_op jit(solution)/shard_map/ppermute | solution.py:87
  81.3 5.6 %collective-permute-start.26 = (bf16[32,1024]{1,0:T(8,128)(2,1)S(1)}, bf16[32,1024]{1,0:T(8,128)(2,1)S(1)}, u32[]{:S(2)}, u32[]{:S(2)}) collective-permute-start(bf16[32,1024]{1,0:T(8,128)(2,1)S(1)} %get-tuple-element.124.refs_0_), channel_id=1, source_target_pairs={{0,3},{1,0},{2,1},{3,2},{4,7},{5,4},{6,5},{7,6},{8,11},{9,8},{10,9... | collective-permute-start | bytes 196616 | tf_op jit(solution)/shard_map/ppermute | solution.py:87
  83.4 7.6 %collective-permute-start.10 = (bf16[128,1024]{1,0:T(8,128)(2,1)S(1)}, bf16[128,1024]{1,0:T(8,128)(2,1)S(1)}, u32[]{:S(2)}, u32[]{:S(2)}) collective-permute-start(bf16[128,1024]{1,0:T(8,128)(2,1)S(1)} %shard_map.248.refs_0_.refs_6_.refs_4_), channel_id=1, source_target_pairs={{0,8},{4,12},{8,0},{12,4},{1,9},{5,13},{9,1},{13,5},{2,10},{6,14},... | collective-permute-start | bytes 786440 | tf_op jit(solution)/shard_map/ppermute | solution.py:92
  85.3 11.8 %collective-permute-start.6 = (bf16[1024,256]{1,0:T(8,128)(2,1)S(1)}, bf16[1024,256]{1,0:T(8,128)(2,1)S(1)}, u32[]{:S(2)}, u32[]{:S(2)}) collective-permute-start(bf16[1024,256]{1,0:T(8,128)(2,1)S(1)} %shard_map.247.mine), channel_id=1, source_target_pairs={{0,16},{16,0},{1,17},{17,1},{2,18},{18,2},{3,19},{19,3},{4,20},{20... | collective-permute-start | bytes 1572872 | tf_op jit(solution)/shard_map/ppermute | solution.py:92
  87.5 8.0 %collective-permute-start.27 = (bf16[128,1024]{1,0:T(8,128)(2,1)S(1)}, bf16[128,1024]{1,0:T(8,128)(2,1)S(1)}, u32[]{:S(2)}, u32[]{:S(2)}) collective-permute-start(bf16[128,1024]{1,0:T(8,128)(2,1)S(1)} %shard_map.255.refs_0_), channel_id=1, source_target_pairs={{0,8},{4,12},{8,0},{12,4},{1,9},{5,13},{9,1},{13,5},{2,10},{6,14},... | collective-permute-start | bytes 786440 | tf_op jit(solution)/shard_map/ppermute | solution.py:92
  88.2 7.3 %collective-permute-start.11 = (bf16[128,1024]{1,0:T(8,128)(2,1)S(1)}, bf16[128,1024]{1,0:T(8,128)(2,1)S(1)}, u32[]{:S(2)}, u32[]{:S(2)}) collective-permute-start(bf16[128,1024]{1,0:T(8,128)(2,1)S(1)} %shard_map.248.refs_0_.refs_6_.refs_4_), channel_id=1, source_target_pairs={{0,4},{4,0},{8,12},{12,8},{1,5},{5,1},{9,13},{13,9},{2,6},{6,2},{1... | collective-permute-start | bytes 786440 | tf_op jit(solution)/shard_map/ppermute | solution.py:92
  91.0 4.6 %collective-permute-start.12 = (bf16[128,1024]{1,0:T(8,128)(2,1)S(1)}, bf16[128,1024]{1,0:T(8,128)(2,1)S(1)}, u32[]{:S(2)}, u32[]{:S(2)}) collective-permute-start(bf16[128,1024]{1,0:T(8,128)(2,1)S(1)} %collective-permute-done.10.refs_1_.refs_5_), channel_id=1, source_target_pairs={{0,4},{4,0},{8,12},{12,8},{1,5},{5,1},{9,13},{13,9},{2,6},{6,2},{1... | collective-permute-start | bytes 786440 | tf_op jit(solution)/shard_map/ppermute | solution.py:92
  91.0 7.6 %collective-permute-start.28 = (bf16[128,1024]{1,0:T(8,128)(2,1)S(1)}, bf16[128,1024]{1,0:T(8,128)(2,1)S(1)}, u32[]{:S(2)}, u32[]{:S(2)}) collective-permute-start(bf16[128,1024]{1,0:T(8,128)(2,1)S(1)} %shard_map.255.refs_0_), channel_id=1, source_target_pairs={{0,4},{4,0},{8,12},{12,8},{1,5},{5,1},{9,13},{13,9},{2,6},{6,2},{1... | collective-permute-start | bytes 786440 | tf_op jit(solution)/shard_map/ppermute | solution.py:92
  95.5 3.0 %collective-permute-start.29 = (bf16[128,1024]{1,0:T(8,128)(2,1)S(1)}, bf16[128,1024]{1,0:T(8,128)(2,1)S(1)}, u32[]{:S(2)}, u32[]{:S(2)}) collective-permute-start(bf16[128,1024]{1,0:T(8,128)(2,1)S(1)} %collective-permute-done.27.refs_1_), channel_id=1, source_target_pairs={{0,4},{4,0},{8,12},{12,8},{1,5},{5,1},{9,13},{13,9},{2,6},{6,2},{1... | collective-permute-start | bytes 786440 | tf_op jit(solution)/shard_map/ppermute | solution.py:92
  102.8 8.4 %collective-permute-start.36 = (bf16[128,1024]{1,0:T(8,128)(2,1)S(1)}, bf16[128,1024]{1,0:T(8,128)(2,1)S(1)}, u32[]{:S(2)}, u32[]{:S(2)}) collective-permute-start(bf16[128,1024]{1,0:T(8,128)(2,1)S(1)} %get-tuple-element.148), channel_id=1, source_target_pairs={{0,8},{4,12},{8,0},{12,4},{1,9},{5,13},{9,1},{13,5},{2,10},{6,14},... | collective-permute-start | bytes 786440 | tf_op jit(solution)/shard_map/ppermute | solution.py:92
  111.9 6.6 %collective-permute-start.37 = (bf16[32,1024]{1,0:T(8,128)(2,1)S(1)}, bf16[32,1024]{1,0:T(8,128)(2,1)S(1)}, u32[]{:S(2)}, u32[]{:S(2)}) collective-permute-start(bf16[32,1024]{1,0:T(8,128)(2,1)S(1)} %get-tuple-element.150), channel_id=1, source_target_pairs={{0,1},{1,2},{2,3},{3,0},{4,5},{5,6},{6,7},{7,4},{8,9},{9,10},{10,1... | collective-permute-start | bytes 196616 | tf_op jit(solution)/shard_map/ppermute | solution.py:87
  113.1 7.1 %collective-permute-start.38 = (bf16[32,1024]{1,0:T(8,128)(2,1)S(1)}, bf16[32,1024]{1,0:T(8,128)(2,1)S(1)}, u32[]{:S(2)}, u32[]{:S(2)}) collective-permute-start(bf16[32,1024]{1,0:T(8,128)(2,1)S(1)} %get-tuple-element.151), channel_id=1, source_target_pairs={{0,2},{1,3},{2,0},{3,1},{4,6},{5,7},{6,4},{7,5},{8,10},{9,11},{10,... | collective-permute-start | bytes 196616 | tf_op jit(solution)/shard_map/ppermute | solution.py:87
  113.4 6.8 %collective-permute-start.39 = (bf16[32,1024]{1,0:T(8,128)(2,1)S(1)}, bf16[32,1024]{1,0:T(8,128)(2,1)S(1)}, u32[]{:S(2)}, u32[]{:S(2)}) collective-permute-start(bf16[32,1024]{1,0:T(8,128)(2,1)S(1)} %get-tuple-element.152), channel_id=1, source_target_pairs={{0,3},{1,0},{2,1},{3,2},{4,7},{5,4},{6,5},{7,6},{8,11},{9,8},{10,9... | collective-permute-start | bytes 196616 | tf_op jit(solution)/shard_map/ppermute | solution.py:87
  120.9 6.6 %collective-permute-start.40 = (bf16[32,1024]{1,0:T(8,128)(2,1)S(1)}, bf16[32,1024]{1,0:T(8,128)(2,1)S(1)}, u32[]{:S(2)}, u32[]{:S(2)}) collective-permute-start(bf16[32,1024]{1,0:T(8,128)(2,1)S(1)} %get-tuple-element.155.refs_0_), channel_id=1, source_target_pairs={{0,1},{1,2},{2,3},{3,0},{4,5},{5,6},{6,7},{7,4},{8,9},{9,10},{10,1... | collective-permute-start | bytes 196616 | tf_op jit(solution)/shard_map/ppermute | solution.py:87
  122.5 6.8 %collective-permute-start.41 = (bf16[32,1024]{1,0:T(8,128)(2,1)S(1)}, bf16[32,1024]{1,0:T(8,128)(2,1)S(1)}, u32[]{:S(2)}, u32[]{:S(2)}) collective-permute-start(bf16[32,1024]{1,0:T(8,128)(2,1)S(1)} %get-tuple-element.155.refs_0_), channel_id=1, source_target_pairs={{0,2},{1,3},{2,0},{3,1},{4,6},{5,7},{6,4},{7,5},{8,10},{9,11},{10,... | collective-permute-start | bytes 196616 | tf_op jit(solution)/shard_map/ppermute | solution.py:87
  123.7 5.6 %collective-permute-start.42 = (bf16[32,1024]{1,0:T(8,128)(2,1)S(1)}, bf16[32,1024]{1,0:T(8,128)(2,1)S(1)}, u32[]{:S(2)}, u32[]{:S(2)}) collective-permute-start(bf16[32,1024]{1,0:T(8,128)(2,1)S(1)} %get-tuple-element.155.refs_0_), channel_id=1, source_target_pairs={{0,3},{1,0},{2,1},{3,2},{4,7},{5,4},{6,5},{7,6},{8,11},{9,8},{10,9... | collective-permute-start | bytes 196616 | tf_op jit(solution)/shard_map/ppermute | solution.py:87
  129.9 6.8 %collective-permute-start.43 = (bf16[128,1024]{1,0:T(8,128)(2,1)S(1)}, bf16[128,1024]{1,0:T(8,128)(2,1)S(1)}, u32[]{:S(2)}, u32[]{:S(2)}) collective-permute-start(bf16[128,1024]{1,0:T(8,128)(2,1)S(1)} %shard_map.265.refs_0_), channel_id=1, source_target_pairs={{0,8},{4,12},{8,0},{12,4},{1,9},{5,13},{9,1},{13,5},{2,10},{6,14},... | collective-permute-start | bytes 786440 | tf_op jit(solution)/shard_map/ppermute | solution.py:92
  130.8 11.8 %collective-permute-start.44 = (bf16[128,1024]{1,0:T(8,128)(2,1)S(1)}, bf16[128,1024]{1,0:T(8,128)(2,1)S(1)}, u32[]{:S(2)}, u32[]{:S(2)}) collective-permute-start(bf16[128,1024]{1,0:T(8,128)(2,1)S(1)} %shard_map.265.refs_0_), channel_id=1, source_target_pairs={{0,4},{4,0},{8,12},{12,8},{1,5},{5,1},{9,13},{13,9},{2,6},{6,2},{1... | collective-permute-start | bytes 786440 | tf_op jit(solution)/shard_map/ppermute | solution.py:92
  136.7 5.8 %collective-permute-start.45 = (bf16[128,1024]{1,0:T(8,128)(2,1)S(1)}, bf16[128,1024]{1,0:T(8,128)(2,1)S(1)}, u32[]{:S(2)}, u32[]{:S(2)}) collective-permute-start(bf16[128,1024]{1,0:T(8,128)(2,1)S(1)} %collective-permute-done.43.refs_1_), channel_id=1, source_target_pairs={{0,4},{4,0},{8,12},{12,8},{1,5},{5,1},{9,13},{13,9},{2,6},{6,2},{1... | collective-permute-start | bytes 786440 | tf_op jit(solution)/shard_map/ppermute | solution.py:92
  137.4 71.1 %collective-permute-start.55 = (bf16[512,1024]{1,0:T(8,128)(2,1)S(1)}, bf16[512,1024]{1,0:T(8,128)(2,1)S(1)}, u32[]{:S(2)}, u32[]{:S(2)}) collective-permute-start(bf16[512,1024]{1,0:T(8,128)(2,1)S(1)} %shard_map.271), channel_id=1, source_target_pairs={{0,16},{16,0},{1,17},{17,1},{2,18},{18,2},{3,19},{19,3},{4,20},{20... | collective-permute-start | bytes 3145736 | tf_op jit(solution)/shard_map/ppermute | solution.py:92
  140.1 34.3 %collective-permute-start.60 = (bf16[1040,256]{1,0:T(8,128)(2,1)S(1)}, bf16[1040,256]{1,0:T(8,128)(2,1)S(1)}, u32[]{:S(2)}, u32[]{:S(2)}) collective-permute-start(bf16[1040,256]{1,0:T(8,128)(2,1)S(1)} %get-tuple-element.179), channel_id=1, source_target_pairs={{0,16},{16,0},{1,17},{17,1},{2,18},{18,2},{3,19},{19,3},{4,20},{20... | collective-permute-start | bytes 1597448 | tf_op jit(solution)/shard_map/ppermute | solution.py:92
  145.1 32.6 %collective-permute-start.46 = (bf16[256,1024]{1,0:T(8,128)(2,1)S(1)}, bf16[256,1024]{1,0:T(8,128)(2,1)S(1)}, u32[]{:S(2)}, u32[]{:S(2)}) collective-permute-start(bf16[256,1024]{1,0:T(8,128)(2,1)S(1)} %get-tuple-element.157), channel_id=1, source_target_pairs={{0,4},{4,0},{8,12},{12,8},{1,5},{5,1},{9,13},{13,9},{2,6},{6,2},{1... | collective-permute-start | bytes 1572872 | tf_op jit(solution)/shard_map/ppermute | solution.py:92
  146.1 34.6 %collective-permute-start.30 = (bf16[256,1024]{1,0:T(8,128)(2,1)S(1)}, bf16[256,1024]{1,0:T(8,128)(2,1)S(1)}, u32[]{:S(2)}, u32[]{:S(2)}) collective-permute-start(bf16[256,1024]{1,0:T(8,128)(2,1)S(1)} %get-tuple-element.128), channel_id=1, source_target_pairs={{0,4},{4,0},{8,12},{12,8},{1,5},{5,1},{9,13},{13,9},{2,6},{6,2},{1... | collective-permute-start | bytes 1572872 | tf_op jit(solution)/shard_map/ppermute | solution.py:92
  175.1 8.5 %collective-permute-start.61 = (bf16[272,256]{1,0:T(8,128)(2,1)S(1)}, bf16[272,256]{1,0:T(8,128)(2,1)S(1)}, u32[]{:S(2)}, u32[]{:S(2)}) collective-permute-start(bf16[272,256]{1,0:T(8,128)(2,1)S(1)} %get-tuple-element.181), channel_id=1, source_target_pairs={{0,1},{1,2},{2,3},{3,0},{4,5},{5,6},{6,7},{7,4},{8,9},{9,10},{10,1... | collective-permute-start | bytes 417800 | tf_op jit(solution)/shard_map/ppermute | solution.py:87
  177.6 10.6 %collective-permute-start.62 = (bf16[272,256]{1,0:T(8,128)(2,1)S(1)}, bf16[272,256]{1,0:T(8,128)(2,1)S(1)}, u32[]{:S(2)}, u32[]{:S(2)}) collective-permute-start(bf16[272,256]{1,0:T(8,128)(2,1)S(1)} %get-tuple-element.182), channel_id=1, source_target_pairs={{0,2},{1,3},{2,0},{3,1},{4,6},{5,7},{6,4},{7,5},{8,10},{9,11},{10,... | collective-permute-start | bytes 417800 | tf_op jit(solution)/shard_map/ppermute | solution.py:87
  177.6 10.6 %collective-permute-start.63 = (bf16[272,256]{1,0:T(8,128)(2,1)S(1)}, bf16[272,256]{1,0:T(8,128)(2,1)S(1)}, u32[]{:S(2)}, u32[]{:S(2)}) collective-permute-start(bf16[272,256]{1,0:T(8,128)(2,1)S(1)} %get-tuple-element.183), channel_id=1, source_target_pairs={{0,3},{1,0},{2,1},{3,2},{4,7},{5,4},{6,5},{7,6},{8,11},{9,8},{10,9... | collective-permute-start | bytes 417800 | tf_op jit(solution)/shard_map/ppermute | solution.py:87
  180.8 9.4 %collective-permute-start.47 = (bf16[128,1024]{1,0:T(8,128)(2,1)S(1)}, bf16[128,1024]{1,0:T(8,128)(2,1)S(1)}, u32[]{:S(2)}, u32[]{:S(2)}) collective-permute-start(bf16[128,1024]{1,0:T(8,128)(2,1)S(1)} %get-tuple-element.159), channel_id=1, source_target_pairs={{0,8},{4,12},{8,0},{12,4},{1,9},{5,13},{9,1},{13,5},{2,10},{6,14},... | collective-permute-start | bytes 786440 | tf_op jit(solution)/shard_map/ppermute | solution.py:92
  183.6 12.2 %collective-permute-start.31 = (bf16[128,1024]{1,0:T(8,128)(2,1)S(1)}, bf16[128,1024]{1,0:T(8,128)(2,1)S(1)}, u32[]{:S(2)}, u32[]{:S(2)}) collective-permute-start(bf16[128,1024]{1,0:T(8,128)(2,1)S(1)} %get-tuple-element.130), channel_id=1, source_target_pairs={{0,8},{4,12},{8,0},{12,4},{1,9},{5,13},{9,1},{13,5},{2,10},{6,14},... | collective-permute-start | bytes 786440 | tf_op jit(solution)/shard_map/ppermute | solution.py:92
  189.4 41.2 %collective-permute-start.64 = (bf16[1024,256]{1,0:T(8,128)(2,1)S(1)}, bf16[1024,256]{1,0:T(8,128)(2,1)S(1)}, u32[]{:S(2)}, u32[]{:S(2)}) collective-permute-start(bf16[1024,256]{1,0:T(8,128)(2,1)S(1)} %get-tuple-element.184.mine), channel_id=1, source_target_pairs={{0,16},{16,0},{1,17},{17,1},{2,18},{18,2},{3,19},{19,3},{4,20},{20... | collective-permute-start | bytes 1572872 | tf_op jit(solution)/shard_map/ppermute | solution.py:92
  191.1 7.0 %collective-permute-start.48 = (bf16[144,256]{1,0:T(8,128)(2,1)S(1)}, bf16[144,256]{1,0:T(8,128)(2,1)S(1)}, u32[]{:S(2)}, u32[]{:S(2)}) collective-permute-start(bf16[144,256]{1,0:T(8,128)(2,1)S(1)} %get-tuple-element.163), channel_id=1, source_target_pairs={{0,1},{1,2},{2,3},{3,0},{4,5},{5,6},{6,7},{7,4},{8,9},{9,10},{10,1... | collective-permute-start | bytes 221192 | tf_op jit(solution)/shard_map/ppermute | solution.py:87
  194.6 17.2 %collective-permute-start.54 = (bf16[528,192]{1,0:T(8,128)(2,1)S(1)}, bf16[528,192]{1,0:T(8,128)(2,1)S(1)}, u32[]{:S(2)}, u32[]{:S(2)}) collective-permute-start(bf16[528,192]{1,0:T(8,128)(2,1)S(1)} %get-tuple-element.168.joined), channel_id=1, source_target_pairs={{0,16},{16,0},{1,17},{17,1},{2,18},{18,2},{3,19},{19,3},{4,20},{20... | collective-permute-start | bytes 608264 | tf_op jit(solution)/shard_map/ppermute | solution.py:92
  195.8 5.6 %collective-permute-start.49 = (bf16[144,256]{1,0:T(8,128)(2,1)S(1)}, bf16[144,256]{1,0:T(8,128)(2,1)S(1)}, u32[]{:S(2)}, u32[]{:S(2)}) collective-permute-start(bf16[144,256]{1,0:T(8,128)(2,1)S(1)} %get-tuple-element.164), channel_id=1, source_target_pairs={{0,2},{1,3},{2,0},{3,1},{4,6},{5,7},{6,4},{7,5},{8,10},{9,11},{10,... | collective-permute-start | bytes 221192 | tf_op jit(solution)/shard_map/ppermute | solution.py:87
  198.0 13.7 %collective-permute-start.56 = (bf16[64,1024]{1,0:T(8,128)(2,1)S(1)}, bf16[64,1024]{1,0:T(8,128)(2,1)S(1)}, u32[]{:S(2)}, u32[]{:S(2)}) collective-permute-start(bf16[64,1024]{1,0:T(8,128)(2,1)S(1)} %shard_map.272.out_a), channel_id=1, source_target_pairs={{0,16},{16,0},{1,17},{17,1},{2,18},{18,2},{3,19},{19,3},{4,20},{20... | collective-permute-start | bytes 393224 | tf_op jit(solution)/shard_map/ppermute | solution.py:92
  201.4 4.4 %collective-permute-start.50 = (bf16[144,256]{1,0:T(8,128)(2,1)S(1)}, bf16[144,256]{1,0:T(8,128)(2,1)S(1)}, u32[]{:S(2)}, u32[]{:S(2)}) collective-permute-start(bf16[144,256]{1,0:T(8,128)(2,1)S(1)} %get-tuple-element.165), channel_id=1, source_target_pairs={{0,3},{1,0},{2,1},{3,2},{4,7},{5,4},{6,5},{7,6},{8,11},{9,8},{10,9... | collective-permute-start | bytes 221192 | tf_op jit(solution)/shard_map/ppermute | solution.py:87
  205.8 11.1 %collective-permute-start.32 = (bf16[128,256]{1,0:T(8,128)(2,1)S(1)}, bf16[128,256]{1,0:T(8,128)(2,1)S(1)}, u32[]{:S(2)}, u32[]{:S(2)}) collective-permute-start(bf16[128,256]{1,0:T(8,128)(2,1)S(1)} %get-tuple-element.133), channel_id=1, source_target_pairs={{0,1},{1,2},{2,3},{3,0},{4,5},{5,6},{6,7},{7,4},{8,9},{9,10},{10,1... | collective-permute-start | bytes 196616 | tf_op jit(solution)/shard_map/ppermute | solution.py:87
  208.5 10.8 %collective-permute-start.33 = (bf16[128,256]{1,0:T(8,128)(2,1)S(1)}, bf16[128,256]{1,0:T(8,128)(2,1)S(1)}, u32[]{:S(2)}, u32[]{:S(2)}) collective-permute-start(bf16[128,256]{1,0:T(8,128)(2,1)S(1)} %get-tuple-element.134), channel_id=1, source_target_pairs={{0,2},{1,3},{2,0},{3,1},{4,6},{5,7},{6,4},{7,5},{8,10},{9,11},{10,... | collective-permute-start | bytes 196616 | tf_op jit(solution)/shard_map/ppermute | solution.py:87
  211.7 5.5 %collective-permute-start.51 = (f32[8,256]{1,0:T(8,128)S(1)}, f32[8,256]{1,0:T(8,128)S(1)}, u32[]{:S(2)}, u32[]{:S(2)}) collective-permute-start(f32[8,256]{1,0:T(8,128)S(1)} %get-tuple-element.167), channel_id=1, source_target_pairs={{0,4},{4,0},{8,12},{12,8},{1,5},{5,1},{9,13},{13,9},{2,6},{6,2},{1... | collective-permute-start | bytes 24584 | tf_op jit(solution)/shard_map/ppermute | solution.py:92
  213.2 19.3 %collective-permute-start.57 = (bf16[272,256]{1,0:T(8,128)(2,1)S(1)}, bf16[272,256]{1,0:T(8,128)(2,1)S(1)}, u32[]{:S(2)}, u32[]{:S(2)}) collective-permute-start(bf16[272,256]{1,0:T(8,128)(2,1)S(1)} %get-tuple-element.170), channel_id=1, source_target_pairs={{0,1},{1,2},{2,3},{3,0},{4,5},{5,6},{6,7},{7,4},{8,9},{9,10},{10,1... | collective-permute-start | bytes 417800 | tf_op jit(solution)/shard_map/ppermute | solution.py:87
  216.8 15.7 %collective-permute-start.58 = (bf16[272,256]{1,0:T(8,128)(2,1)S(1)}, bf16[272,256]{1,0:T(8,128)(2,1)S(1)}, u32[]{:S(2)}, u32[]{:S(2)}) collective-permute-start(bf16[272,256]{1,0:T(8,128)(2,1)S(1)} %get-tuple-element.171), channel_id=1, source_target_pairs={{0,2},{1,3},{2,0},{3,1},{4,6},{5,7},{6,4},{7,5},{8,10},{9,11},{10,... | collective-permute-start | bytes 417800 | tf_op jit(solution)/shard_map/ppermute | solution.py:87
  217.2 15.3 %collective-permute-start.59 = (bf16[272,256]{1,0:T(8,128)(2,1)S(1)}, bf16[272,256]{1,0:T(8,128)(2,1)S(1)}, u32[]{:S(2)}, u32[]{:S(2)}) collective-permute-start(bf16[272,256]{1,0:T(8,128)(2,1)S(1)} %get-tuple-element.172), channel_id=1, source_target_pairs={{0,3},{1,0},{2,1},{3,2},{4,7},{5,4},{6,5},{7,6},{8,11},{9,8},{10,9... | collective-permute-start | bytes 417800 | tf_op jit(solution)/shard_map/ppermute | solution.py:87
  219.3 3.7 %collective-permute-start.52 = (f32[8,256]{1,0:T(8,128)S(1)}, f32[8,256]{1,0:T(8,128)S(1)}, u32[]{:S(2)}, u32[]{:S(2)}) collective-permute-start(f32[8,256]{1,0:T(8,128)S(1)} %add.19), channel_id=1, source_target_pairs={{0,8},{4,12},{8,0},{12,4},{1,9},{5,13},{9,1},{13,5},{2,10},{6,14},... | collective-permute-start | bytes 24584 | tf_op jit(solution)/shard_map/ppermute | solution.py:92
  222.9 5.6 %collective-permute-start.34 = (bf16[128,256]{1,0:T(8,128)(2,1)S(1)}, bf16[128,256]{1,0:T(8,128)(2,1)S(1)}, u32[]{:S(2)}, u32[]{:S(2)}) collective-permute-start(bf16[128,256]{1,0:T(8,128)(2,1)S(1)} %get-tuple-element.135), channel_id=1, source_target_pairs={{0,3},{1,0},{2,1},{3,2},{4,7},{5,4},{6,5},{7,6},{8,11},{9,8},{10,9... | collective-permute-start | bytes 196616 | tf_op jit(solution)/shard_map/ppermute | solution.py:87
  228.5 6.3 %collective-permute-start.53 = (f32[8,256]{1,0:T(8,128)S(1)}, f32[8,256]{1,0:T(8,128)S(1)}, u32[]{:S(2)}, u32[]{:S(2)}) collective-permute-start(f32[8,256]{1,0:T(8,128)S(1)} %add.20), channel_id=1, source_target_pairs={{0,16},{16,0},{1,17},{17,1},{2,18},{18,2},{3,19},{19,3},{4,20},{20... | collective-permute-start | bytes 24584 | tf_op jit(solution)/shard_map/ppermute | solution.py:92
  (10 other events, 69.0 us)
